TPU v7x, 512 devices: a whole 4x8x8 slice. The times are simulated.
512 devices in a mesh: expert: 64 (over x, z, core), dp: 8 (over y).
Axes of the slice: x: 4, y: 8, z: 8, core: 2. Of those that a mesh axis runs over, the one named last changes fastest.
Arguments:
- tokens: bfloat16 [65536, 2048], P(('expert', 'dp')), may hold values from -6 to 6
- upstream: bfloat16 [65536, 2048], P(('expert', 'dp')), may hold values from -6 to 6
- expert_ids: int32 [65536, 2], P(('expert', 'dp')), may hold values from 0 to 63, all different within a row; in each aligned block of 128 rows (0 to 127, 128 to 255, ...) at most 8 rows name the same one
- route_weight: bfloat16 [65536, 2], P(('expert', 'dp')), may hold values from 0.099609375 to 1
- placement: int32 [64], replicated, may hold values from 0 to 63, each once
- swap_pair: int32 [32], replicated, may hold values 0 or 1
- expert_state: bfloat16 [64, 2048, 1024], P('expert', 'dp'), may hold values from -0.125 to 0.125
- first_moment: bfloat16 [64, 2048, 1024], P('expert', 'dp'), may hold values from -60 to 60
- second_moment: bfloat16 [64, 2048, 1024], P('expert', 'dp'), may hold values from 10 to 1000
Outputs:
- token_grad: bfloat16 [65536, 2048], P(('expert', 'dp'))
- weight_grad: bfloat16 [65536, 2], P(('expert', 'dp'))
- new_state: bfloat16 [64, 2048, 1024], P('expert', 'dp')
- new_first: bfloat16 [64, 2048, 1024], P('expert', 'dp')
- new_second: bfloat16 [64, 2048, 1024], P('expert', 'dp')
Inputs may be any that keep to these rules, and one draw needn't show every extreme that they name: `expert_ids`: among the rows of one device no expert is named by more than 8 routes, and some expert reaches 8; a token's 2 experts differ.
All inputs are finite; a program needn't handle non-finite values.
Results may differ from a plain program's by a relative error of at most 0.0075.
Values may be sent and summed in bfloat16 or wider, within the bound.
A program may use at most 64 MiB of HBM per device.

v0:
```python
import math

import jax
import jax.numpy as jnp
from jax import lax
from jax.sharding import PartitionSpec as P

corr_one = 1.0 - math.exp(1000.0 * math.log(0.9))
corr_two = 1.0 - math.exp(1000.0 * math.log(0.999))


def partner_2(value, axis, stride):
    mask = 2**stride
    pairs = [(source, source ^ mask) for source in range(lax.axis_size(axis))]
    return lax.ppermute(value, axis, pairs)


def silu_grad(value):
    sig = jax.nn.sigmoid(value)
    return sig * (1.0 + value * (1.0 - sig))


def trade_state(stacked, own_flag):
    lanes_count = lax.axis_size("expert")
    partner = partner_2(stacked, "expert", lanes_count.bit_length() - 2)
    return jnp.where(own_flag == 1, partner, stacked)


def adam_update(weights, first, second, grad):
    m_next = 0.9 * first.astype(jnp.float32) + 0.1 * grad
    v_next = 0.999 * second.astype(jnp.float32) + 0.001 * grad * grad
    update = m_next / corr_one / (jnp.sqrt(v_next / corr_two) + 1e-08)
    w_old = weights.astype(jnp.float32)
    w_next = w_old - 0.001 * (update + 0.1 * w_old)
    return jnp.stack(
        [w_next.astype(jnp.bfloat16), m_next.astype(jnp.bfloat16), v_next.astype(jnp.bfloat16)]
    )


def shards(
    tokens,
    upstream,
    expert_ids,
    route_weight,
    placement,
    swap_pair,
    expert_state,
    first_moment,
    second_moment,
):
    f32 = jnp.float32
    bf16 = jnp.bfloat16
    lanes_count = lax.axis_size("expert")
    half = lanes_count // 2
    rows = tokens.shape[0]
    top = expert_ids.shape[1]
    width = tokens.shape[1]
    hidden_units = expert_state.shape[2] // 2
    capacity = 2 * rows * top // lanes_count
    halves = jnp.arange(half, dtype=jnp.int32)
    lanes = jnp.arange(lanes_count, dtype=jnp.int32)
    own_index = lax.axis_index("expert")
    own_flag = jnp.sum(jnp.where(halves == own_index % half, swap_pair, 0))
    stacked = jnp.stack([expert_state, first_moment, second_moment])
    match_half = (placement % half)[:, None] == halves[None, :]
    moved = jnp.sum(jnp.where(match_half, swap_pair[None, :], 0), 1)
    home = jnp.where(moved == 1, placement ^ half, placement)
    stacked = trade_state(stacked, own_flag)
    flat_ids = expert_ids.reshape(-1)
    match_expert = flat_ids[:, None] == lanes[None, :]
    dest = jnp.sum(jnp.where(match_expert, home[None, :], 0), 1)
    dest_hot = (dest[:, None] == lanes[None, :]).astype(jnp.int32)
    earlier = jnp.cumsum(dest_hot, 0) - dest_hot
    slot = jnp.sum(earlier * dest_hot, 1)
    position = dest * capacity + slot
    x_buf = (
        jnp.zeros((lanes_count * capacity, width), bf16)
        .at[position]
        .set(jnp.repeat(tokens, top, axis=0))
    )
    y_buf = (
        jnp.zeros((lanes_count * capacity, width), bf16)
        .at[position]
        .set(jnp.repeat(upstream, top, axis=0))
    )
    w_buf = jnp.zeros((lanes_count * capacity,), bf16).at[position].set(route_weight.reshape(-1))
    x_buf = x_buf.reshape(lanes_count, capacity, width)
    y_buf = y_buf.reshape(lanes_count, capacity, width)
    w_buf = w_buf.reshape(lanes_count, capacity)
    x_recv, y_recv, w_recv = (
        lax.all_to_all(x_buf, "expert", split_axis=0, concat_axis=0, tiled=True),
        lax.all_to_all(y_buf, "expert", split_axis=0, concat_axis=0, tiled=True),
        lax.all_to_all(w_buf, "expert", split_axis=0, concat_axis=0, tiled=True),
    )
    full = lax.all_gather(stacked[0], "dp", axis=1, tiled=True)[0]
    w_up = full[:, :hidden_units]
    w_down = full[:, hidden_units:]
    x_rows = x_recv.reshape(-1, width)
    hid = jnp.dot(x_rows, w_up, preferred_element_type=f32)
    act = jax.nn.silu(hid).astype(bf16)
    out = lax.dot_general(act, w_down, (((1,), (1,)), ((), ())), preferred_element_type=f32)
    y_rows = y_recv.reshape(-1, width)
    slot_dw = jnp.sum(y_rows.astype(f32) * out, 1).astype(bf16)
    grad_rows = (w_recv.reshape(-1)[:, None].astype(f32) * y_rows.astype(f32)).astype(bf16)
    back = jnp.dot(grad_rows, w_down, preferred_element_type=f32)
    dh = (back * silu_grad(hid)).astype(bf16)
    slot_dx = lax.dot_general(
        dh, w_up, (((1,), (1,)), ((), ())), preferred_element_type=f32
    ).astype(bf16)
    returned_dx, returned_dw = (
        lax.all_to_all(
            slot_dx.reshape(lanes_count, capacity, width),
            "expert",
            split_axis=0,
            concat_axis=0,
            tiled=True,
        ),
        lax.all_to_all(
            slot_dw.reshape(lanes_count, capacity),
            "expert",
            split_axis=0,
            concat_axis=0,
            tiled=True,
        ),
    )
    route_dx = returned_dx.reshape(-1, width)[position]
    token_grad = jnp.sum(route_dx.reshape(rows, top, width).astype(f32), 1).astype(bf16)
    weight_grad = returned_dw.reshape(-1)[position].reshape(rows, top)
    up_part = lax.dot_general(x_rows, dh, (((0,), (0,)), ((), ())), preferred_element_type=f32)
    down_part = lax.dot_general(
        grad_rows, act, (((0,), (0,)), ((), ())), preferred_element_type=f32
    )
    grad = lax.psum_scatter(
        jnp.concatenate([up_part, down_part], 1).astype(jnp.bfloat16),
        "dp",
        scatter_dimension=0,
        tiled=True,
    ).astype(jnp.float32)[None]
    updated = adam_update(stacked[0], stacked[1], stacked[2], grad)
    return (token_grad, weight_grad, updated[0], updated[1], updated[2])


def solution(mesh):
    in_specs = (
        P(("expert", "dp"), None),
        P(("expert", "dp"), None),
        P(("expert", "dp"), None),
        P(("expert", "dp"), None),
        P(),
        P(),
        P("expert", "dp", None),
        P("expert", "dp", None),
        P("expert", "dp", None),
    )
    out_specs = (
        P(("expert", "dp"), None),
        P(("expert", "dp"), None),
        P("expert", "dp", None),
        P("expert", "dp", None),
        P("expert", "dp", None),
    )
    return jax.shard_map(shards, mesh=mesh, in_specs=in_specs, out_specs=out_specs, check_vma=False)
```

profile of v0, /device:TPU:1, one launch (start us, length us, event | category | flops | bytes accessed | tf_op | source)
XLA Modules:
  0.0 280.3 jit_solution(14328996724233734354)
XLA Ops:
  7.2 1.3 copy.46
  8.5 1.2 copy.47
  9.8 0.2 copy.48
  10.0 1.3 pad_maximum_fusion.1
  11.3 5.5 %collective-permute-start = (bf16[3,1,256,1024]{2,3,1,0:T(8,128)(2,1)}, bf16[3,1,256,1024]{2,3,1,0:T(8,128)(2,1)}, u32[]{:S(2)}, u32[]{:S(2)}) collective-permute-start(bf16[3,1,256,1024]{2,3,1,0:T(8,128)(2,1)} %pad_maximum_fusion.1), channel_id=1, source_target_pairs={{0,256},{8,264},{16,272},{24,280},{32,288},{40,296},{48,304},{56,3... | collective-permute-start | bytes 4718600 | tf_op jit(solution)/shard_map/ppermute | solution.py:15
  17.6 0.6 reduce-window.6
  18.2 0.2 slice_reduce_fusion
  18.6 2.2 scatter_custom_fusion
  20.8 0.7 all_to_all.25
  21.5 12.4 %all-to-all-start = ((bf16[64,1,8]{2,1,0:T(2,128)(2,1)}), bf16[64,1,8]{2,1,0:T(2,128)(2,1)S(1)}, u32[]{:S(2)}, u32[]{:S(2)}) async-start(bf16[64,1,8]{2,1,0:T(2,128)(2,1)} %all_to_all.25), calls=%async_computation | async-start | bytes 65536 | tf_op jit(solution)/shard_map/all_to_all | solution.py:93
  33.9 0.6 broadcast_in_dim.57
  34.5 1.2 reshape.205
  35.8 4.4 %scatter_custom_fusion.2 = bf16[512,2048]{1,0:T(8,128)(2,1)} fusion(s32[256]{0:T(256)S(1)} %bitcast.87, bf16[256,2048]{1,0:T(8,128)(2,1)} %reshape.205, bf16[]{:T(256)} %constant.20.clone.1), kind=kCustom, calls=%fused_computation.37 | custom fusion | bytes 2097664 | tf_op jit(solution)/shard_map/scatter | solution.py:79
  40.2 12.2 %all-to-all-done = bf16[64,1,8]{2,1,0:T(2,128)(2,1)S(1)} async-done(((bf16[64,1,8]{2,1,0:T(2,128)(2,1)}), bf16[64,1,8]{2,1,0:T(2,128)(2,1)S(1)}, u32[]{:S(2)}, u32[]{:S(2)}) %all-to-all-start) | async-done | bytes 1056 | tf_op jit(solution)/shard_map/all_to_all | solution.py:93
  52.4 14.2 %all-to-all-start.2 = ((bf16[64,8,2048]{2,1,0:T(8,128)(2,1)}), bf16[64,8,2048]{2,1,0:T(8,128)(2,1)}, u32[]{:S(2)}, u32[]{:S(2)}) async-start(bf16[64,8,2048]{2,1,0:T(8,128)(2,1)} %bitcast.10), calls=%async_computation.2 | async-start | bytes 4194304 | tf_op jit(solution)/shard_map/all_to_all | solution.py:91
  66.6 0.2 all-gather.3.cloned.1.call-start
  66.8 0.6 fusion.37
  68.1 1.7 broadcast_select_fusion
  69.8 1.1 copy-done
  70.9 0.8 slice.34
  71.8 0.6 broadcast_in_dim.55
  72.4 0.4 reshape.197
  72.9 3.8 %scatter_custom_fusion.1 = bf16[512,2048]{1,0:T(8,128)(2,1)} fusion(s32[256]{0:T(256)S(1)} %bitcast.88, bf16[256,2048]{1,0:T(8,128)(2,1)S(1)} %reshape.197, bf16[]{:T(256)} %constant.20.clone.1), kind=kCustom, calls=%fused_computation.39 | custom fusion | bytes 2097154 | tf_op jit(solution)/shard_map/scatter | solution.py:84
  76.7 41.0 %all-to-all-done.2 = bf16[64,8,2048]{2,1,0:T(8,128)(2,1)} async-done(((bf16[64,8,2048]{2,1,0:T(8,128)(2,1)}), bf16[64,8,2048]{2,1,0:T(8,128)(2,1)}, u32[]{:S(2)}, u32[]{:S(2)}) %all-to-all-start.2) | async-done | bytes 2097184 | tf_op jit(solution)/shard_map/all_to_all | solution.py:91
  117.7 5.8 %all-to-all-start.1 = ((bf16[64,8,2048]{2,1,0:T(8,128)(2,1)}), bf16[64,8,2048]{2,1,0:T(8,128)(2,1)S(1)}, u32[]{:S(2)}, u32[]{:S(2)}) async-start(bf16[64,8,2048]{2,1,0:T(8,128)(2,1)} %bitcast.4), calls=%async_computation.1 | async-start | bytes 4194304 | tf_op jit(solution)/shard_map/all_to_all | solution.py:92
  123.8 10.9 %all-gather.3.cloned.1.call-done = bf16[1,1,2048,1024]{2,3,1,0:T(8,128)(2,1)} async-done(((bf16[1,1,256,1024]{2,3,1,0:T(8,128)(2,1)}), bf16[1,1,2048,1024]{2,3,1,0:T(8,128)(2,1)}) %all-gather.3.cloned.1.call-update) | async-done | bytes 4194320 | tf_op jit(solution)/shard_map/all_gather | solution.py:95
  134.7 4.5 %fusion.4 = f32[512,512]{1,0:T(8,128)} fusion(bf16[64,8,2048]{2,1,0:T(8,128)(2,1)} %all-to-all-done.2, bf16[2048,1024]{0,1:T(8,128)(2,1)} %bitcast.91), kind=kOutput, calls=%fused_computation.15 | convolution fusion | flops 1073741824 | bytes 5242880 | tf_op jit(solution)/shard_map/dot_general | solution.py:99
  139.2 35.6 %all-to-all-done.1 = bf16[64,8,2048]{2,1,0:T(8,128)(2,1)S(1)} async-done(((bf16[64,8,2048]{2,1,0:T(8,128)(2,1)}), bf16[64,8,2048]{2,1,0:T(8,128)(2,1)S(1)}, u32[]{:S(2)}, u32[]{:S(2)}) %all-to-all-start.1) | async-done | bytes 2097184 | tf_op jit(solution)/shard_map/all_to_all | solution.py:92
  174.8 3.4 %fusion.14 = bf16[512,512]{1,0:T(8,128)(2,1)S(1)} fusion(bf16[2048,1024]{0,1:T(8,128)(2,1)} %bitcast.92, f32[512,512]{1,0:T(8,128)} %fusion.4, bf16[64,8,2048]{2,1,0:T(8,128)(2,1)S(1)} %all-to-all-done.1, f32[512]{0:T(512)S(1)} %reshape.166), kind=kOutput, calls=%fused_computation.29 | convolution fusion | flops 1079246848 | bytes 5769216 | tf_op jit(solution)/shard_map/dot_general | solution.py:105
  178.2 1.5 convolution_convert_fusion
  179.7 2.9 %convolution_convert_fusion.1 = bf16[2048,512]{0,1:T(8,128)(2,1)S(1)} fusion(bf16[512,512]{1,0:T(8,128)(2,1)S(1)} %fusion.14, bf16[64,8,2048]{2,1,0:T(8,128)(2,1)} %all-to-all-done.2), kind=kOutput, calls=%fused_computation.11 | convolution fusion | flops 1074790400 | bytes 4718592 | tf_op jit(solution)/shard_map/dot_general | solution.py:129
  182.6 2.6 pad_maximum_fusion
  185.2 3.3 %fusion.1 = bf16[512]{0:T(512)(128)(2,1)S(1)} fusion(bf16[64,8,2048]{2,1,0:T(8,128)(2,1)S(1)} %all-to-all-done.1, bf16[2048,1024]{0,1:T(8,128)(2,1)} %bitcast.93, f32[512,512]{1,0:T(8,128)} %fusion.4), kind=kOutput, calls=%fused_computation.8 | convolution fusion | flops 1078197760 | bytes 5243904 | tf_op jit(solution)/shard_map/dot_general | solution.py:101
  188.5 0.7 convert_element_type.118
  189.2 5.8 %all-to-all-start.4 = ((bf16[64,1,8]{2,1,0:T(2,128)(2,1)}), bf16[64,1,8]{2,1,0:T(2,128)(2,1)S(1)}, u32[]{:S(2)}, u32[]{:S(2)}) async-start(bf16[64,1,8]{2,1,0:T(2,128)(2,1)} %convert_element_type.118), calls=%async_computation.4 | async-start | bytes 65536 | tf_op jit(solution)/shard_map/all_to_all | solution.py:118
  195.0 4.6 %fusion.2 = bf16[64,8,2048]{2,1,0:T(8,128)(2,1)} fusion(bf16[512,512]{1,0:T(8,128)(2,1)S(1)} %fusion.14, bf16[2048,1024]{0,1:T(8,128)(2,1)} %bitcast.94), kind=kOutput, calls=%fused_computation.13 | convolution fusion | flops 1074790400 | bytes 4718592 | tf_op jit(solution)/shard_map/dot_general | solution.py:107
  199.6 4.6 %all-to-all-done.4 = bf16[64,1,8]{2,1,0:T(2,128)(2,1)S(1)} async-done(((bf16[64,1,8]{2,1,0:T(2,128)(2,1)}), bf16[64,1,8]{2,1,0:T(2,128)(2,1)S(1)}, u32[]{:S(2)}, u32[]{:S(2)}) %all-to-all-start.4) | async-done | bytes 1056 | tf_op jit(solution)/shard_map/all_to_all | solution.py:118
  204.2 5.4 %all-to-all-start.3 = ((bf16[64,8,2048]{2,1,0:T(8,128)(2,1)}), bf16[64,8,2048]{2,1,0:T(8,128)(2,1)S(1)}, u32[]{:S(2)}, u32[]{:S(2)}) async-start(bf16[64,8,2048]{2,1,0:T(8,128)(2,1)} %fusion.2), calls=%async_computation.3 | async-start | bytes 4194304 | tf_op jit(solution)/shard_map/all_to_all | solution.py:111
  209.8 1.9 gather_fusion.1
  211.9 0.6 copy.50
  212.5 48.3 %all-to-all-done.3 = bf16[64,8,2048]{2,1,0:T(8,128)(2,1)S(1)} async-done(((bf16[64,8,2048]{2,1,0:T(8,128)(2,1)}), bf16[64,8,2048]{2,1,0:T(8,128)(2,1)S(1)}, u32[]{:S(2)}, u32[]{:S(2)}) %all-to-all-start.3) | async-done | bytes 2097184 | tf_op jit(solution)/shard_map/all_to_all | solution.py:111
  260.9 1.4 gather_fusion
  262.2 1.6 reshape.163
  263.8 4.6 %reduce_sum.61 = bf16[128,2048]{1,0:T(8,128)(2,1)} reduce(bf16[128,2,2048]{2,1,0:T(2,128)(2,1)} %reshape.163, bf16[]{:T(256)} %constant.20.clone.1), dimensions={1}, to_apply=%region_9.10 | reduce | flops 262144 | bytes 1572866 | tf_op jit(solution)/shard_map/reduce_sum | solution.py:127
  268.4 2.1 fusion.30
  270.5 1.0 copy.53
  271.5 1.0 copy.52
  272.5 1.0 copy.51
  (44 shorter events, 1.6 us)
Async XLA Ops:
  7.2 2.6 copy-start.4
  9.7 7.1 %copy-start.7 = (s32[64]{0:T(128)S(1)}, s32[64]{0:T(128)}, u32[]{:S(2)}) copy-start(s32[64]{0:T(128)} %param.13) | copy-start | bytes 772
  9.8 7.1 %copy-start.6 = (bf16[128,2]{0,1:T(2,128)(2,1)S(1)}, bf16[128,2]{0,1:T(2,128)(2,1)}, u32[]{:S(2)}) copy-start(bf16[128,2]{0,1:T(2,128)(2,1)} %param.12) | copy-start | bytes 1540
  9.8 7.4 %copy-start.5 = (s32[128,2]{0,1:T(2,128)S(1)}, s32[128,2]{0,1:T(2,128)}, u32[]{:S(2)}) copy-start(s32[128,2]{0,1:T(2,128)} %param.11) | copy-start | bytes 3076
  9.8 7.6 %copy-start.8 = (s32[32]{0:T(128)S(1)}, s32[32]{0:T(128)}, u32[]{:S(2)}) copy-start(s32[32]{0:T(128)} %param.14) | copy-start | bytes 388
  10.0 23.9 %copy-start.2 = (bf16[128,2048]{1,0:T(8,128)(2,1)S(1)}, bf16[128,2048]{1,0:T(8,128)(2,1)}, u32[]{:S(2)}) copy-start(bf16[128,2048]{1,0:T(8,128)(2,1)} %param.9) | copy-start | bytes 1572868
  11.3 56.8 %collective-permute-start = (bf16[3,1,256,1024]{2,3,1,0:T(8,128)(2,1)}, bf16[3,1,256,1024]{2,3,1,0:T(8,128)(2,1)}, u32[]{:S(2)}, u32[]{:S(2)}) collective-permute-start(bf16[3,1,256,1024]{2,3,1,0:T(8,128)(2,1)} %pad_maximum_fusion.1), channel_id=1, source_target_pairs={{0,256},{8,264},{16,272},{24,280},{32,288},{40,296},{48,304},{56,3... | collective-permute-start | bytes 4718600 | tf_op jit(solution)/shard_map/ppermute | solution.py:15
  21.5 30.9 %all-to-all-start = ((bf16[64,1,8]{2,1,0:T(2,128)(2,1)}), bf16[64,1,8]{2,1,0:T(2,128)(2,1)S(1)}, u32[]{:S(2)}, u32[]{:S(2)}) async-start(bf16[64,1,8]{2,1,0:T(2,128)(2,1)} %all_to_all.25), calls=%async_computation | async-start | bytes 65536 | tf_op jit(solution)/shard_map/all_to_all | solution.py:93
  52.4 65.3 %all-to-all-start.2 = ((bf16[64,8,2048]{2,1,0:T(8,128)(2,1)}), bf16[64,8,2048]{2,1,0:T(8,128)(2,1)}, u32[]{:S(2)}, u32[]{:S(2)}) async-start(bf16[64,8,2048]{2,1,0:T(8,128)(2,1)} %bitcast.10), calls=%async_computation.2 | async-start | bytes 4194304 | tf_op jit(solution)/shard_map/all_to_all | solution.py:91
  66.6 68.1 %all-gather.3.cloned.1.call-start = ((), (), s32[]{:S(2)}) async-start(), calls=%async_computation.7 | async-start | bytes 4718592 | tf_op jit(solution)/shard_map/all_gather | solution.py:95
  68.1 3.7 %copy-start.3 = (bf16[128,2048]{1,0:T(8,128)(2,1)S(1)}, bf16[128,2048]{1,0:T(8,128)(2,1)}, u32[]{:S(2)}) copy-start(bf16[128,2048]{1,0:T(8,128)(2,1)} %param.10) | copy-start | bytes 1572868
  69.8 1.1 copy-start
  117.7 57.1 %all-to-all-start.1 = ((bf16[64,8,2048]{2,1,0:T(8,128)(2,1)}), bf16[64,8,2048]{2,1,0:T(8,128)(2,1)S(1)}, u32[]{:S(2)}, u32[]{:S(2)}) async-start(bf16[64,8,2048]{2,1,0:T(8,128)(2,1)} %bitcast.4), calls=%async_computation.1 | async-start | bytes 4194304 | tf_op jit(solution)/shard_map/all_to_all | solution.py:92
  123.5 144.8 %reduce-scatter.2.cloned.1.call-start = ((), (), s32[]{:S(2)}) async-start(), calls=%async_computation.6 | async-start | bytes 4718592 | tf_op jit(solution)/shard_map/reduce_scatter | solution.py:133
  174.8 3.4 %copy-start.9 = (f32[512,512]{1,0:T(8,128)S(1)}, f32[512,512]{1,0:T(8,128)}, u32[]{:S(2)}) copy-start(f32[512,512]{1,0:T(8,128)} %fusion.4) | copy-start | bytes 3145732
  189.2 15.0 %all-to-all-start.4 = ((bf16[64,1,8]{2,1,0:T(2,128)(2,1)}), bf16[64,1,8]{2,1,0:T(2,128)(2,1)S(1)}, u32[]{:S(2)}, u32[]{:S(2)}) async-start(bf16[64,1,8]{2,1,0:T(2,128)(2,1)} %convert_element_type.118), calls=%async_computation.4 | async-start | bytes 65536 | tf_op jit(solution)/shard_map/all_to_all | solution.py:118
  204.2 56.7 %all-to-all-start.3 = ((bf16[64,8,2048]{2,1,0:T(8,128)(2,1)}), bf16[64,8,2048]{2,1,0:T(8,128)(2,1)S(1)}, u32[]{:S(2)}, u32[]{:S(2)}) async-start(bf16[64,8,2048]{2,1,0:T(8,128)(2,1)} %fusion.2), calls=%async_computation.3 | async-start | bytes 4194304 | tf_op jit(solution)/shard_map/all_to_all | solution.py:111
  262.2 6.2 %copy-start.1 = (bf16[3,1,256,1024]{2,3,1,0:T(8,128)(2,1)S(1)}, bf16[3,1,256,1024]{2,3,1,0:T(8,128)(2,1)}, u32[]{:S(2)}) copy-start(bf16[3,1,256,1024]{2,3,1,0:T(8,128)(2,1)} %copy-done) | copy-start | bytes 4718596
Sparse Core Ops, SparseCore 0:
  71.9 62.7 all-gather.2
  185.3 54.1 reduce-scatter.1
where the time goes:
time: 281 us; the launch traced here: 280 us
  waiting for transfers between devices  153 us (54%)
  starting transfers between devices  49.3 us (18%)
  local copies, waits for them, and re-layouts  29.1 us (10%)
  matrix products  20.2 us (7%)
  between operations  15 us (5%)
  other arithmetic  14 us (5%)
    all_to_all x1, waiting for transfers between devices, shards(): lax.all_to_all(slot_dx.reshape(lanes_count, capacity, width), 'expert', s...  48.3 us
    all_to_all x1, waiting for transfers between devices, shards(): lax.all_to_all(x_buf, 'expert', split_axis=0, concat_axis=0, tiled=True)  41 us
    all_to_all x1, waiting for transfers between devices, shards(): lax.all_to_all(y_buf, 'expert', split_axis=0, concat_axis=0, tiled=True)  35.6 us
    all_to_all x1, starting transfers between devices, shards(): lax.all_to_all(x_buf, 'expert', split_axis=0, concat_axis=0, tiled=True)  14.2 us
    all_to_all x1, starting transfers between devices, shards(): lax.all_to_all(w_buf, 'expert', split_axis=0, concat_axis=0, tiled=True)  12.4 us
    all_to_all x1, waiting for transfers between devices, shards(): lax.all_to_all(w_buf, 'expert', split_axis=0, concat_axis=0, tiled=True)  12.2 us
    all_gather x1, waiting for transfers between devices, shards(): full = lax.all_gather(stacked[0], 'dp', axis=1, tiled=True)[0]  10.9 us
    unnamed x29, local copies, waits for them, and re-layouts  7.8 us
  transfers between devices with their start and end apart: 8, of which 6 were waited for; matrix products, arithmetic and copies ran while one was open for 15% of the time, Pallas kernels for 0%

commit v1 on v0

v1 whole, which is shorter than its diff:
```python
import functools
import math

import jax
import jax.numpy as jnp
from jax import lax
from jax.experimental import pallas as pl
from jax.experimental.pallas import tpu as pltpu
from jax.sharding import PartitionSpec as P

corr_one = 1.0 - math.exp(1000.0 * math.log(0.9))
corr_two = 1.0 - math.exp(1000.0 * math.log(0.999))

NX, NZ, NC = 4, 8, 2
CAP = 8
LANES = 128
MESH = pl.DeviceIdType.MESH
F32 = jnp.float32
BF16 = jnp.bfloat16


def iota(shape, dim):
    return lax.broadcasted_iota(jnp.int32, shape, dim)


def tiles(total, tile, body):
    if total <= tile:
        body(0)
        return

    def step(i, carry):
        body(pl.multiple_of(i * tile, tile))
        return carry

    lax.fori_loop(0, total // tile, step, 0)


def kernel(
    sizes,
    tok, up, meta, homec, flag, w_in, m_in, v_in,
    tg, dwo, grad, w_sel, m_got, v_got,
    xa, ya, mt, w_got, wfull, sx, sy, rx, ry, act_all, dh_all,
    dxs, dr, sr, fr, rs_send, rs_recv,
    z_send, z_recv, mt_send, mt_recv, sw_send, sw_recv, y_send, y_recv,
    x_send, x_recv, r_send, r_recv, b_send, b_recv, rs_ssem, rs_rsem, local_sem,
):
    ny, rows, width, hidden, wide = sizes
    ng = NX * NC
    hz, hy = NZ // 2, ny // 2
    chunk = 2 * CAP * ng
    part = width // ny
    half_rows = rows // 2
    e = lax.axis_index("expert")
    d = lax.axis_index("dp")
    c = lax.rem(e, NC)
    z = lax.rem(e // NC, NZ)
    x = e // (NC * NZ)
    g = x * NC + c

    def zdev(k):
        return {"expert": (x * NZ + lax.rem(z + k + NZ, NZ)) * NC + c}

    def gdev(k):
        return {"expert": (lax.div(k, NC) * NZ + z) * NC + lax.rem(k, NC)}

    def ydev(k):
        return {"dp": lax.rem(d + k + ny, ny)}

    def remote(src, dst, ssem, rsem, dev):
        return pltpu.make_async_remote_copy(
            src_ref=src, dst_ref=dst, send_sem=ssem, recv_sem=rsem, device_id=dev, device_id_type=MESH
        )

    barrier = pltpu.get_barrier_semaphore()
    for k in range(1, NZ):
        pl.semaphore_signal(barrier, inc=1, device_id=zdev(k), device_id_type=MESH)
    for k in range(1, ng):
        pl.semaphore_signal(barrier, inc=1, device_id=gdev(lax.rem(g + k, ng)), device_id_type=MESH)
    for k in (1, -1):
        pl.semaphore_signal(barrier, inc=1, device_id=ydev(k), device_id_type=MESH)
    pl.semaphore_wait(barrier, NZ - 1 + ng - 1 + 2)

    own = (tok, up)
    every = (xa, ya)

    def z_copy(t, way, step, sending):
        sign = 1 if way == 0 else -1
        back = step - 1 if sending else step
        block = lax.rem(z - sign * back + 2 * NZ, NZ)
        start = pl.multiple_of(block * rows, rows)
        low, size = (0, rows) if step < hz else (way * half_rows, half_rows)
        dst = every[t].at[pl.ds(start + low, size)]
        src = own[t].at[pl.ds(low, size)] if step == 1 else dst
        return remote(src, dst, z_send.at[t, way, step - 1], z_recv.at[t, way, step - 1], zdev(sign))

    def z_start(t, step):
        for way in (0, 1):
            z_copy(t, way, step, True).start()

    def z_wait(t, step):
        for way in (0, 1):
            z_copy(t, way, step, False).wait_recv()

    half = NX * NZ * NC // 2
    partner = {"expert": lax.rem(e + half, 2 * half)}
    swaps = [
        remote(src, dst, sw_send.at[i], sw_recv.at[i], partner)
        for i, (src, dst) in enumerate(((w_in, w_got), (m_in, m_got), (v_in, v_got)))
    ]

    def y_copy(way, step, sending):
        sign = 1 if way == 0 else -1
        back = step - 1 if sending else step
        block = lax.rem(d - sign * back + 2 * ny, ny)
        start = pl.multiple_of(block * part, part)
        low, size = (0, part) if step < hy else (way * (part // 2), part // 2)
        ref = wfull.at[pl.ds(start + low, size)]
        return remote(ref, ref, y_send.at[way, step - 1], y_recv.at[way, step - 1], ydev(sign))

    def y_start(step):
        for way in (0, 1):
            y_copy(way, step, True).start()

    def y_wait(step):
        for way in (0, 1):
            y_copy(way, step, False).wait_recv()

    def mt_copy(k, sending):
        block = z if sending else lax.rem(z - k + NZ, NZ)
        ref = mt.at[pl.ds(pl.multiple_of(block * 8, 8), 8)]
        return remote(ref, ref, mt_send.at[k - 1], mt_recv.at[k - 1], zdev(k))

    def positions():
        experts = homec.shape[0]
        ids0, ids1 = meta[0:1, :], meta[1:2, :]
        each = iota((experts, rows), 0).astype(F32)
        one0, one1 = ids0 == each, ids1 == each
        named = jnp.where(one0 | one1, 1.0, 0.0).astype(BF16)
        before = jnp.where(iota((rows, rows), 0) < iota((rows, rows), 1), 1.0, 0.0).astype(BF16)
        earlier = jnp.dot(named, before, preferred_element_type=F32)
        place = homec[...] * CAP + earlier
        pos0 = jnp.sum(jnp.where(one0, place, 0.0), 0, keepdims=True)
        pos1 = jnp.sum(jnp.where(one1, place, 0.0), 0, keepdims=True)
        line = iota((8, rows), 0)
        tile = jnp.where(line == 0, pos0, jnp.where(line == 1, pos1, meta[...]))
        mt[pl.ds(pl.multiple_of(z * 8, 8), 8), :] = tile

    def sources(p):
        if p == 0:
            return z, lax.rem(z + hz, NZ)
        return lax.rem(z + p, NZ), lax.rem(z - p + NZ, NZ)

    def pack(p, t):
        line = iota((chunk, rows), 0)
        group, side, slot = line // (2 * CAP), (line // CAP) % 2, line % CAP
        aim = (((group // NC) * NZ + z) * NC + group % NC) * CAP + slot
        hots, starts = [], []
        for s, block in enumerate(sources(p)):
            tile = mt[pl.ds(pl.multiple_of(block * 8, 8), 8), :]
            want = jnp.where(side == s, aim, -1).astype(F32)
            hit0, hit1 = tile[0:1, :] == want, tile[1:2, :] == want
            if t == 0:
                hot = jnp.where(hit0 | hit1, 1.0, 0.0)
            else:
                hot = jnp.where(hit0, tile[2:3, :], 0.0) + jnp.where(hit1, tile[3:4, :], 0.0)
            hots.append(hot.astype(BF16))
            starts.append(pl.multiple_of(block * rows, rows))
        out, got, buf = (sx, rx, xa) if t == 0 else (sy, ry, ya)
        mine = pl.ds(pl.multiple_of(p * chunk + g * 2 * CAP, 2 * CAP), 2 * CAP)

        def body(start):
            cols = pl.ds(start, min(512, width))
            packed = jnp.dot(hots[0], buf[pl.ds(starts[0], rows), cols], preferred_element_type=F32)
            packed += jnp.dot(hots[1], buf[pl.ds(starts[1], rows), cols], preferred_element_type=F32)
            out[pl.ds(p * chunk, chunk), cols] = packed.astype(BF16)

        tiles(width, 512, body)
        got[mine, :] = out[mine, :]

    def x_copy(p, t, k, sending):
        other = lax.rem(g + k, ng) if sending else lax.rem(g - k + ng, ng)
        src, dst = ((sx, rx), (sy, ry))[t]
        there = pl.ds(pl.multiple_of(p * chunk + other * 2 * CAP, 2 * CAP), 2 * CAP)
        here = pl.ds(pl.multiple_of(p * chunk + g * 2 * CAP, 2 * CAP), 2 * CAP)
        if sending:
            return remote(src.at[there], dst.at[here], x_send.at[t, p, k - 1], x_recv.at[t, p, k - 1], gdev(other))
        return remote(src.at[here], dst.at[there], x_send.at[t, p, k - 1], x_recv.at[t, p, k - 1], gdev(other))

    def peers(body):
        def step(k, carry):
            body(k)
            return carry

        lax.fori_loop(1, ng, step, 0)

    def x_start(p, t):
        peers(lambda k: x_copy(p, t, k, True).start())

    def x_wait(p, t):
        peers(lambda k: x_copy(p, t, k, False).wait_recv())

    def compute(p):
        at = pl.ds(p * chunk, chunk)
        hid = jnp.dot(rx[at, :], wfull[:, 0:hidden], preferred_element_type=F32)
        sig = 1.0 / (1.0 + jnp.exp(-hid))
        act = (hid * sig).astype(BF16)
        back = jnp.dot(ry[at, :], wfull[:, hidden:], preferred_element_type=F32)
        dh = (back * (sig * (1.0 + hid * (1.0 - sig)))).astype(BF16)
        act_all[at, :] = act
        dh_all[at, :] = dh
        weighted = jnp.sum(act.astype(F32) * back, 1, keepdims=True)
        dxs[at, width:] = jnp.broadcast_to(weighted, (chunk, LANES)).astype(BF16)

        def body(start):
            tile = wfull[pl.ds(start, min(512, width)), 0:hidden]
            dx = lax.dot_general(dh_all[at, :], tile, (((1,), (1,)), ((), ())), preferred_element_type=F32)
            dxs[at, pl.ds(start, min(512, width))] = dx.astype(BF16)

        tiles(width, 512, body)
        mine = pl.ds(pl.multiple_of(p * chunk + g * 2 * CAP, 2 * CAP), 2 * CAP)
        dr[mine, :] = dxs[mine, :]

    def r_copy(p, k, sending):
        other = lax.rem(g + k, ng) if sending else lax.rem(g - k + ng, ng)
        there = pl.ds(pl.multiple_of(p * chunk + other * 2 * CAP, 2 * CAP), 2 * CAP)
        here = pl.ds(pl.multiple_of(p * chunk + g * 2 * CAP, 2 * CAP), 2 * CAP)
        if sending:
            return remote(dxs.at[there], dr.at[here], r_send.at[p, k - 1], r_recv.at[p, k - 1], gdev(other))
        return remote(dxs.at[here], dr.at[there], r_send.at[p, k - 1], r_recv.at[p, k - 1], gdev(other))

    def r_start(p):
        peers(lambda k: r_copy(p, k, True).start())

    side_rows = CAP * ng

    def b_copy(p, s, sending):
        away = hz if p == 0 else (p if s == 0 else -p)
        block = z if sending else lax.rem(z - away + NZ, NZ)
        src = sr.at[pl.ds((2 * p + s) * side_rows, side_rows)]
        dst = fr.at[pl.ds(pl.multiple_of(block * side_rows, side_rows), side_rows)]
        return remote(src, dst, b_send.at[p, s], b_recv.at[p, s], zdev(away))

    def relay(p):
        peers(lambda k: r_copy(p, k, False).wait_recv())
        to, frm = iota((chunk, chunk), 0), iota((chunk, chunk), 1)
        side, group, slot = to // side_rows, (to // CAP) % ng, to % CAP
        move = jnp.where(frm == group * 2 * CAP + side * CAP + slot, 1.0, 0.0).astype(BF16)

        def body(start, size=min(512, width)):
            cols = pl.ds(start, size)
            moved = jnp.dot(move, dr[pl.ds(p * chunk, chunk), cols], preferred_element_type=F32)
            sr[pl.ds(p * chunk, chunk), cols] = moved.astype(BF16)

        tiles(width, 512, body)
        body(width, LANES)
        if p == 0:
            fr[pl.ds(pl.multiple_of(z * side_rows, side_rows), side_rows), :] = sr[0:side_rows, :]
            b_copy(0, 1, True).start()
        else:
            for s in (0, 1):
                b_copy(p, s, True).start()

    def own_part(block, h):
        cols = pl.ds(pl.multiple_of(block * part, part), part)
        left, right = ((rx, dh_all), (ry, act_all))[h]
        return lax.dot_general(
            left[:, cols], right[...], (((0,), (0,)), ((), ())), preferred_element_type=F32
        )

    def rs_copy(way, step, h):
        sign = 1 if way == 0 else -1
        return remote(
            rs_send.at[way, step - 1, h], rs_recv.at[way, step - 1, h],
            rs_ssem.at[way, step - 1, h], rs_rsem.at[way, step - 1, h], ydev(sign),
        )

    def rs_halves(way, step):
        return (way,) if step == 1 else (0, 1)

    def rs_step(step):
        for h in (0, 1):
            for way in (0, 1):
                if h not in rs_halves(way, step):
                    continue
                sign = 1 if way == 0 else -1
                block = lax.rem(d + sign * (hy + 1 - step) + ny, ny)
                total = own_part(block, h)
                if step > 1 and h in rs_halves(way, step - 1):
                    rs_copy(way, step - 1, h).wait_recv()
                    total += rs_recv[way, step - 2, h].astype(F32)
                rs_send[way, step - 1, h] = total.astype(BF16)
                rs_copy(way, step, h).start()

    def rs_last():
        for h in (0, 1):
            total = own_part(d, h)
            for way in (0, 1):
                if h in rs_halves(way, hy):
                    rs_copy(way, hy, h).wait_recv()
                    total += rs_recv[way, hy - 1, h].astype(F32)
            grad[:, h * hidden : (h + 1) * hidden] = total

    def finish():
        for p in range(hz):
            for s in (0, 1):
                if (p, s) != (0, 0):
                    b_copy(p, s, False).wait_recv()
        tile = mt[pl.ds(pl.multiple_of(z * 8, 8), 8), :]
        lines = side_rows * NZ
        line = iota((lines, rows), 0)
        plane, group, slot = line // side_rows, (line // CAP) % ng, line % CAP
        want = ((((group // NC) * NZ + plane) * NC + group % NC) * CAP + slot).astype(F32)
        hit0, hit1 = tile[0:1, :] == want, tile[1:2, :] == want
        both = jnp.where(hit0 | hit1, 1.0, 0.0).astype(BF16)
        dims = (((0,), (0,)), ((), ()))

        def body(start):
            cols = pl.ds(start, min(512, width))
            tg[:, cols] = lax.dot_general(both, fr[:, cols], dims, preferred_element_type=F32).astype(BF16)

        tiles(width, 512, body)
        lane = iota((rows, LANES), 1)
        sums = [
            lax.dot_general(
                jnp.where(hit, 1.0, 0.0).astype(BF16), fr[:, width:], dims, preferred_element_type=F32
            )
            for hit in (hit0, hit1)
        ]
        dwo[...] = jnp.where(lane == 0, sums[0], sums[1])

    z_start(0, 1)
    swaps[0].start()
    z_start(1, 1)
    positions()
    for k in range(1, NZ):
        mt_copy(k, True).start()
    xa[pl.ds(pl.multiple_of(z * rows, rows), rows), :] = tok[...]
    ya[pl.ds(pl.multiple_of(z * rows, rows), rows), :] = up[...]

    def state_in():
        swaps[0].wait_recv()
        here = pl.ds(pl.multiple_of(d * part, part), part)
        chosen = jnp.where(flag[0:1, :] == 1.0, w_got[...].astype(F32), w_in[...].astype(F32)).astype(BF16)
        wfull[here, :] = chosen
        w_sel[...] = chosen
        y_start(1)
        swaps[1].start()
        swaps[2].start()

    def metas_in():
        for k in range(1, NZ):
            mt_copy(k, False).wait_recv()

    done_y = 0
    for step in range(1, hz + 1):
        for t in (0, 1):
            z_wait(t, step)
            if step < hz:
                z_start(t, step + 1)
            if step == 1 and t == 0:
                state_in()
                metas_in()
        if step < hz:
            if step <= hy:
                y_wait(step)
                done_y = step
                if step < hy:
                    y_start(step + 1)
            for t in (0, 1):
                pack(step, t)
                x_start(step, t)
    while done_y < hy:
        done_y += 1
        y_wait(done_y)
        if done_y < hy:
            y_start(done_y + 1)
    for t in (0, 1):
        pack(0, t)
        x_start(0, t)
    for p in list(range(1, hz)) + [0]:
        for t in (0, 1):
            x_wait(p, t)
        compute(p)
        r_start(p)
    rs_step(1)
    for p in list(range(1, hz)):
        relay(p)
    if hy > 1:
        rs_step(2)
    relay(0)
    for step in range(3, hy + 1):
        rs_step(step)
    finish()
    rs_last()

    for t in (0, 1):
        for way in (0, 1):
            for step in range(1, hz + 1):
                z_copy(t, way, step, True).wait_send()
    for way in (0, 1):
        for step in range(1, hy + 1):
            y_copy(way, step, True).wait_send()
            for h in rs_halves(way, step):
                rs_copy(way, step, h).wait_send()
    for k in range(1, NZ):
        mt_copy(k, True).wait_send()
    for p in range(hz):
        for t in (0, 1):
            peers(lambda k: x_copy(p, t, k, True).wait_send())
        peers(lambda k: r_copy(p, k, True).wait_send())
        for s in (0, 1):
            if (p, s) != (0, 0):
                b_copy(p, s, True).wait_send()
    swaps[0].wait_send()
    for i in (1, 2):
        swaps[i].wait()


def exchange(tokens, upstream, meta, homec, flag, w_in, m_in, v_in):
    ny = lax.axis_size("dp")
    rows, width = tokens.shape
    part, both = w_in.shape
    hidden = both // 2
    ng = NX * NC
    hz, hy = NZ // 2, ny // 2
    chunk = 2 * CAP * ng
    lines = hz * chunk
    wide = width + LANES
    vmem = pl.BlockSpec(memory_space=pltpu.VMEM)
    any_ = pl.BlockSpec(memory_space=pl.ANY)
    dma = pltpu.SemaphoreType.DMA
    return pl.pallas_call(
        functools.partial(kernel, (ny, rows, width, hidden, wide)),
        name="exchange",
        out_shape=(
            jax.ShapeDtypeStruct((rows, width), BF16),
            jax.ShapeDtypeStruct((rows, LANES), F32),
            jax.ShapeDtypeStruct((part, both), F32),
            jax.ShapeDtypeStruct((part, both), BF16),
            jax.ShapeDtypeStruct((part, both), BF16),
            jax.ShapeDtypeStruct((part, both), BF16),
        ),
        in_specs=[vmem] * 6 + [any_] * 2,
        out_specs=(vmem,) * 4 + (any_,) * 2,
        scratch_shapes=[
            pltpu.VMEM((NZ * rows, width), BF16),
            pltpu.VMEM((NZ * rows, width), BF16),
            pltpu.VMEM((NZ * 8, rows), F32),
            pltpu.VMEM((part, both), BF16),
            pltpu.VMEM((width, both), BF16),
            pltpu.VMEM((lines, width), BF16),
            pltpu.VMEM((lines, width), BF16),
            pltpu.VMEM((lines, width), BF16),
            pltpu.VMEM((lines, width), BF16),
            pltpu.VMEM((lines, hidden), BF16),
            pltpu.VMEM((lines, hidden), BF16),
            pltpu.VMEM((lines, wide), BF16),
            pltpu.VMEM((lines, wide), BF16),
            pltpu.VMEM((lines, wide), BF16),
            pltpu.VMEM((lines, wide), BF16),
            pltpu.VMEM((2, hy, 2, part, hidden), BF16),
            pltpu.VMEM((2, hy, 2, part, hidden), BF16),
            dma((2, 2, hz)), dma((2, 2, hz)),
            dma((NZ - 1,)), dma((NZ - 1,)),
            dma((3,)), dma((3,)),
            dma((2, hy)), dma((2, hy)),
            dma((2, hz, ng - 1)), dma((2, hz, ng - 1)),
            dma((hz, ng - 1)), dma((hz, ng - 1)),
            dma((hz, 2)), dma((hz, 2)),
            dma((2, hy, 2)), dma((2, hy, 2)),
            dma((1,)),
        ],
        compiler_params=pltpu.CompilerParams(
            collective_id=0, has_side_effects=True, vmem_limit_bytes=60 * 1024 * 1024
        ),
    )(tokens, upstream, meta, homec, flag, w_in, m_in, v_in)


def adam_update(weights, first, second, grad):
    m_next = 0.9 * first.astype(F32) + 0.1 * grad
    v_next = 0.999 * second.astype(F32) + 0.001 * grad * grad
    update = m_next / corr_one / (jnp.sqrt(v_next / corr_two) + 1e-08)
    w_old = weights.astype(F32)
    w_next = w_old - 0.001 * (update + 0.1 * w_old)
    return w_next.astype(BF16), m_next.astype(BF16), v_next.astype(BF16)


def shards(
    tokens,
    upstream,
    expert_ids,
    route_weight,
    placement,
    swap_pair,
    expert_state,
    first_moment,
    second_moment,
):
    lanes_count = lax.axis_size("expert")
    half = lanes_count // 2
    rows, top = expert_ids.shape
    both = expert_state.shape[2]
    halves = jnp.arange(half, dtype=jnp.int32)
    own_index = lax.axis_index("expert")
    own_flag = jnp.sum(jnp.where(halves == own_index % half, swap_pair, 0))
    match_half = (placement % half)[:, None] == halves[None, :]
    moved = jnp.sum(jnp.where(match_half, swap_pair[None, :], 0), 1)
    home = jnp.where(moved == 1, placement ^ half, placement)
    homec = jnp.broadcast_to(home.astype(F32)[:, None], (lanes_count, rows))
    flag = jnp.broadcast_to(own_flag.astype(F32), (8, both))
    meta = jnp.concatenate(
        [expert_ids.T.astype(F32), route_weight.T.astype(F32), jnp.zeros((8 - 2 * top, rows), F32)], 0
    )
    token_grad, weighted, grad, w_sel, m_got, v_got = exchange(
        tokens, upstream, meta, homec, flag, expert_state[0], first_moment[0], second_moment[0]
    )
    weight_grad = (weighted[:, :top] / route_weight.astype(F32)).astype(BF16)
    swapped = own_flag == 1
    m_sel = jnp.where(swapped, m_got, first_moment[0])
    v_sel = jnp.where(swapped, v_got, second_moment[0])
    w_new, m_new, v_new = adam_update(w_sel, m_sel, v_sel, grad)
    return (token_grad, weight_grad, w_new[None], m_new[None], v_new[None])


def solution(mesh):
    in_specs = (
        P(("expert", "dp"), None),
        P(("expert", "dp"), None),
        P(("expert", "dp"), None),
        P(("expert", "dp"), None),
        P(),
        P(),
        P("expert", "dp", None),
        P("expert", "dp", None),
        P("expert", "dp", None),
    )
    out_specs = (
        P(("expert", "dp"), None),
        P(("expert", "dp"), None),
        P("expert", "dp", None),
        P("expert", "dp", None),
        P("expert", "dp", None),
    )
    return jax.shard_map(shards, mesh=mesh, in_specs=in_specs, out_specs=out_specs, check_vma=False)
```

time: 281 us -> 190 us (0.68)
  Pallas kernels: 0 us -> 176 us
  waiting for transfers between devices: 153 us -> 0 us
  starting transfers between devices: 49.3 us -> 0 us
  local copies, waits for them, and re-layouts: 29.1 us -> 5.66 us
  matrix products: 20.2 us -> 0 us
  between operations: 15 us -> 2 us
  other arithmetic: 14 us -> 6.03 us
    pallas_call x0 -> x1, Pallas kernels: none -> 176 us  [exchange(): pl.pallas_call(functools.partial(kernel, (ny, rows, width, hidden, wide))...]
    all_to_all x5 -> x0, waiting for transfers between devices: 142 us -> none  [the longest x1 48.3 us: shards(): lax.all_to_all(slot_dx.reshape(lanes_count, capacity, width), 'expert', s...]
    all_to_all x5 -> x0, starting transfers between devices: 43.6 us -> none  [the longest x1 14.2 us: shards(): lax.all_to_all(x_buf, 'expert', split_axis=0, concat_axis=0, tiled=True)]
    dot_general x6 -> x0, matrix products: 20.2 us -> none  [the longest x1 4.61 us: shards(): lax.dot_general(dh, w_up, (((1,), (1,)), ((), ())), preferred_element_typ...]
    all_gather x1 -> x0, waiting for transfers between devices: 10.9 us -> none  [shards(): full = lax.all_gather(stacked[0], 'dp', axis=1, tiled=True)[0]]
    scatter x3 -> x0, local copies, waits for them, and re-layouts: 10.4 us -> none  [the longest x1 4.42 us: shards(): x_buf = jnp.zeros((lanes_count * capacity, width), bf16).at[position].set...]
    ppermute x1 -> x0, starting transfers between devices: 5.47 us -> none  [partner_2(): return lax.ppermute(value, axis, pairs)]
    reduce_sum x3 -> x0, other arithmetic: 4.77 us -> none  [the longest x1 4.57 us: shards(): jnp.sum(route_dx.reshape(rows, top, width).astype(f32), 1).astype(bf16)]
  transfers between devices with their start and end apart: 8 -> 0, of which waited for: 6 -> 0; matrix products, arithmetic and copies ran while one was open for 15% -> 0% of each run, Pallas kernels for 0% -> 0%
where the time goes in v1:
time: 190 us
  Pallas kernels  176 us (93%)
  other arithmetic  6.03 us (3%)
  local copies, waits for them, and re-layouts  5.66 us (3%)
  between operations  2 us (1%)
    pallas_call x1, Pallas kernels, exchange(): pl.pallas_call(functools.partial(kernel, (ny, rows, width, hidden, wide))...  176 us
    broadcast_in_dim x1, other arithmetic, shards(): return (token_grad, weight_grad, w_new[None], m_new[None], v_new[None])  4.1 us

profile of v1, /device:TPU:1, one launch (start us, length us, event | category | flops | bytes accessed | tf_op | source)
XLA Modules:
  0.0 189.9 jit_solution(9070096994627745167)
XLA Ops:
  0.6 0.0 copy-start.5
  0.7 0.6 copy-done.5
  1.3 0.6 fusion.10
  3.2 0.0 copy-start.6
  3.2 0.6 copy-done.6
  3.9 0.1 select_reduce_fusion
  4.0 0.0 copy-start.3
  4.0 0.1 pad.2.clone
  4.1 0.6 copy-done.3
  4.7 0.0 copy-start.4
  4.7 0.7 copy-done.4
  5.3 0.7 maximum_maximum_fusion.meta
  6.0 0.7 broadcast_in_dim.43.homec
  6.7 0.6 broadcast_in_dim.45.flag
  7.3 0.0 copy-start
  7.3 0.0 copy-start.1
  7.3 176.2 %exchange.1 = (bf16[128,2048]{1,0:T(8,128)(2,1)}, f32[128,128]{1,0:T(8,128)}, f32[256,1024]{1,0:T(8,128)}, bf16[256,1024]{1,0:T(8,128)(2,1)}, bf16[256,1024]{1,0:T(8,128)(2,1)}, /*index=5*/bf16[256,1024]{1,0:T(8,128)(2,1)}) custom-call(bf16[128,2048]{1,0:T(8,128)(2,1)} %tok.1, bf16[128,2048]{1,0:T(8,128)(2,1)} %up.1, f32[8,128]{1,0:T(8,128)} %maximum_maximum_fusion.meta, ...), custom_call_target="tpu_custom_call" | custom-call | tf_op jit(solution)/shard_map/exchange/pallas_call | solution.py:432
  183.5 0.9 copy.15
  184.4 0.5 fusion.9
  184.9 0.0 copy-done
  184.9 0.0 copy-done.1
  185.0 0.0 copy-start.2
  185.0 4.1 %fusion.6 = (bf16[1,256,1024]{2,1,0:T(8,128)(2,1)}, bf16[1,256,1024]{2,1,0:T(8,128)(2,1)}, bf16[1,256,1024]{2,1,0:T(8,128)(2,1)}) fusion(f32[256,1024]{1,0:T(8,128)} %get-tuple-element.15, bf16[256,1024]{1,0:T(8,128)(2,1)} %get-tuple-element.16, pred[]{:T(512)S(6)} %eq.39, bf16[1,256,1024]{2,1,0:T(8,128)(2,1)S(1)} %copy-done.1, ...), kind=kLoop, calls=%fused_computation.10 | loop fusion | flops 5767168 | bytes 5242881 | tf_op jit(solution)/shard_map/broadcast_in_dim | solution.py:522
  189.1 0.0 copy-done.2
  189.1 0.8 copy.17
  (5 shorter events, 0.0 us)
Async XLA Ops:
  0.6 0.7 copy-start.5
  3.2 0.7 copy-start.6
  4.0 0.7 copy-start.3
  4.7 0.7 copy-start.4
  7.3 177.6 %copy-start = (bf16[1,256,1024]{2,1,0:T(8,128)(2,1)S(1)}, bf16[1,256,1024]{2,1,0:T(8,128)(2,1)}, u32[]{:S(2)}) copy-start(bf16[1,256,1024]{2,1,0:T(8,128)(2,1)} %param.16) | copy-start | bytes 1572868
  7.3 177.6 %copy-start.1 = (bf16[1,256,1024]{2,1,0:T(8,128)(2,1)S(1)}, bf16[1,256,1024]{2,1,0:T(8,128)(2,1)}, u32[]{:S(2)}) copy-start(bf16[1,256,1024]{2,1,0:T(8,128)(2,1)} %param.17) | copy-start | bytes 1572868
  185.0 4.1 %copy-start.2 = (bf16[128,2048]{1,0:T(8,128)(2,1)S(1)}, bf16[128,2048]{1,0:T(8,128)(2,1)}, u32[]{:S(2)}) copy-start(bf16[128,2048]{1,0:T(8,128)(2,1)} %get-tuple-element.25) | copy-start | bytes 1572868

commit v2 on v1

--- a/solution.py
+++ b/solution.py
@@ -39,7 +39,7 @@
     sizes,
     tok, up, meta, homec, flag, w_in, m_in, v_in,
     tg, dwo, grad, w_sel, m_got, v_got,
-    xa, ya, mt, w_got, wfull, sx, sy, rx, ry, act_all, dh_all,
+    xa, ya, p3, r3, r4, mt, w_got, wfull, sx, sy, rx, ry, act_all, dh_all,
     dxs, dr, sr, fr, rs_send, rs_recv,
     z_send, z_recv, mt_send, mt_recv, sw_send, sw_recv, y_send, y_recv,
     x_send, x_recv, r_send, r_recv, b_send, b_recv, rs_ssem, rs_rsem, local_sem,
@@ -49,7 +49,6 @@
     hz, hy = NZ // 2, ny // 2
     chunk = 2 * CAP * ng
     part = width // ny
-    half_rows = rows // 2
     e = lax.axis_index("expert")
     d = lax.axis_index("dp")
     c = lax.rem(e, NC)
@@ -83,15 +82,22 @@
     own = (tok, up)
     every = (xa, ya)
 
+    side_rows = CAP * ng
+    split = side_rows // 2
+
     def z_copy(t, way, step, sending):
         sign = 1 if way == 0 else -1
+        sems = z_send.at[t, way, step - 1], z_recv.at[t, way, step - 1]
+        if step == hz:
+            return remote(
+                r3.at[t, way, pl.ds(side_rows, split)], r4.at[t, pl.ds(way * split, split)], *sems, zdev(sign)
+            )
+        if step == hz - 1:
+            return remote(p3.at[t, way], r3.at[t, way], *sems, zdev(sign))
         back = step - 1 if sending else step
         block = lax.rem(z - sign * back + 2 * NZ, NZ)
-        start = pl.multiple_of(block * rows, rows)
-        low, size = (0, rows) if step < hz else (way * half_rows, half_rows)
-        dst = every[t].at[pl.ds(start + low, size)]
-        src = own[t].at[pl.ds(low, size)] if step == 1 else dst
-        return remote(src, dst, z_send.at[t, way, step - 1], z_recv.at[t, way, step - 1], zdev(sign))
+        dst = every[t].at[pl.ds(pl.multiple_of(block * rows, rows), rows)]
+        return remote(own[t] if step == 1 else dst, dst, *sems, zdev(sign))
 
     def z_start(t, step):
         for way in (0, 1):
@@ -150,28 +156,61 @@
             return z, lax.rem(z + hz, NZ)
         return lax.rem(z + p, NZ), lax.rem(z - p + NZ, NZ)
 
+    def hot_rows(block, want, t):
+        tile = mt[pl.ds(pl.multiple_of(block * 8, 8), 8), :]
+        want = want.astype(F32)
+        hit0, hit1 = tile[0:1, :] == want, tile[1:2, :] == want
+        if t == 0:
+            hot = jnp.where(hit0 | hit1, 1.0, 0.0)
+        else:
+            hot = jnp.where(hit0, tile[2:3, :], 0.0) + jnp.where(hit1, tile[3:4, :], 0.0)
+        return hot.astype(BF16)
+
+    def pack_ahead(t):
+        lines = side_rows + split
+        line = iota((lines, rows), 0)
+        for way in (0, 1):
+            sign = 1 if way == 0 else -1
+            block = lax.rem(z - sign * (hz - 2) + NZ, NZ)
+            later = line >= side_rows
+            inner = jnp.where(later, line - side_rows + way * split, line)
+            group, slot = inner // CAP, inner % CAP
+            near, far = lax.rem(z + sign + NZ, NZ), lax.rem(z + 2 * sign + NZ, NZ)
+            plane = jnp.where(later, far, near)
+            hot = hot_rows(block, (((group // NC) * NZ + plane) * NC + group % NC) * CAP + slot, t)
+            start = pl.multiple_of(block * rows, rows)
+
+            def body(at):
+                cols = pl.ds(at, min(512, width))
+                p3[t, way, :, cols] = jnp.dot(
+                    hot, every[t][pl.ds(start, rows), cols], preferred_element_type=F32
+                ).astype(BF16)
+
+            tiles(width, 512, body)
+
     def pack(p, t):
         line = iota((chunk, rows), 0)
         group, side, slot = line // (2 * CAP), (line // CAP) % 2, line % CAP
         aim = (((group // NC) * NZ + z) * NC + group % NC) * CAP + slot
-        hots, starts = [], []
+        few = iota((chunk, side_rows), 0)
+        spot = (few // (2 * CAP)) * CAP + few % CAP
+        few_side = (few // CAP) % 2
+        hots, lefts = [], []
         for s, block in enumerate(sources(p)):
-            tile = mt[pl.ds(pl.multiple_of(block * 8, 8), 8), :]
-            want = jnp.where(side == s, aim, -1).astype(F32)
-            hit0, hit1 = tile[0:1, :] == want, tile[1:2, :] == want
-            if t == 0:
-                hot = jnp.where(hit0 | hit1, 1.0, 0.0)
+            if p == hz - 1 or (p == 0 and s == 1):
+                hit = (iota((chunk, side_rows), 1) == spot) & (few_side == s)
+                hots.append(jnp.where(hit, 1.0, 0.0).astype(BF16))
+                lefts.append(r4.at[t] if p == 0 else r3.at[t, 1 - s, pl.ds(0, side_rows)])
             else:
-                hot = jnp.where(hit0, tile[2:3, :], 0.0) + jnp.where(hit1, tile[3:4, :], 0.0)
-            hots.append(hot.astype(BF16))
-            starts.append(pl.multiple_of(block * rows, rows))
-        out, got, buf = (sx, rx, xa) if t == 0 else (sy, ry, ya)
+                hots.append(hot_rows(block, jnp.where(side == s, aim, -1), t))
+                lefts.append(every[t].at[pl.ds(pl.multiple_of(block * rows, rows), rows)])
+        out, got = ((sx, rx), (sy, ry))[t]
         mine = pl.ds(pl.multiple_of(p * chunk + g * 2 * CAP, 2 * CAP), 2 * CAP)
 
         def body(start):
             cols = pl.ds(start, min(512, width))
-            packed = jnp.dot(hots[0], buf[pl.ds(starts[0], rows), cols], preferred_element_type=F32)
-            packed += jnp.dot(hots[1], buf[pl.ds(starts[1], rows), cols], preferred_element_type=F32)
+            packed = jnp.dot(hots[0], lefts[0][:, cols], preferred_element_type=F32)
+            packed += jnp.dot(hots[1], lefts[1][:, cols], preferred_element_type=F32)
             out[pl.ds(p * chunk, chunk), cols] = packed.astype(BF16)
 
         tiles(width, 512, body)
@@ -231,8 +270,6 @@
     def r_start(p):
         peers(lambda k: r_copy(p, k, True).start())
 
-    side_rows = CAP * ng
-
     def b_copy(p, s, sending):
         away = hz if p == 0 else (p if s == 0 else -p)
         block = z if sending else lax.rem(z - away + NZ, NZ)
@@ -240,8 +277,11 @@
         dst = fr.at[pl.ds(pl.multiple_of(block * side_rows, side_rows), side_rows)]
         return remote(src, dst, b_send.at[p, s], b_recv.at[p, s], zdev(away))
 
+    def r_wait(p):
+        peers(lambda k: r_copy(p, k, False).wait_recv())
+
     def relay(p):
-        peers(lambda k: r_copy(p, k, False).wait_recv())
+        r_wait(p)
         to, frm = iota((chunk, chunk), 0), iota((chunk, chunk), 1)
         side, group, slot = to // side_rows, (to // CAP) % ng, to % CAP
         move = jnp.where(frm == group * 2 * CAP + side * CAP + slot, 1.0, 0.0).astype(BF16)
@@ -328,14 +368,9 @@
         ]
         dwo[...] = jnp.where(lane == 0, sums[0], sums[1])
 
-    z_start(0, 1)
-    swaps[0].start()
-    z_start(1, 1)
-    positions()
-    for k in range(1, NZ):
-        mt_copy(k, True).start()
-    xa[pl.ds(pl.multiple_of(z * rows, rows), rows), :] = tok[...]
-    ya[pl.ds(pl.multiple_of(z * rows, rows), rows), :] = up[...]
+    def metas_in():
+        for k in range(1, NZ):
+            mt_copy(k, False).wait_recv()
 
     def state_in():
         swaps[0].wait_recv()
@@ -347,44 +382,89 @@
         swaps[1].start()
         swaps[2].start()
 
-    def metas_in():
+    def y_next(step):
+        if step <= hy:
+            y_wait(step)
+            if step < hy:
+                y_start(step + 1)
+
+    def first_copies():
+        positions()
         for k in range(1, NZ):
-            mt_copy(k, False).wait_recv()
-
+            mt_copy(k, True).start()
+        xa[pl.ds(pl.multiple_of(z * rows, rows), rows), :] = tok[...]
+        ya[pl.ds(pl.multiple_of(z * rows, rows), rows), :] = up[...]
+
+    def send_on(t, step):
+        if step == hz - 1:
+            pack_ahead(t)
+        z_start(t, step)
+
+    swaps[0].start()
+    if hz > 2:
+        z_start(0, 1)
+        z_start(1, 1)
+        first_copies()
+    else:
+        first_copies()
+        metas_in()
+        send_on(0, 1)
+        send_on(1, 1)
     done_y = 0
-    for step in range(1, hz + 1):
+    for step in range(1, hz - 1):
+        z_wait(0, step)
+        if step == 1:
+            metas_in()
+        send_on(0, step + 1)
+        if step == 1:
+            state_in()
+        else:
+            done_y += 1
+            y_next(done_y)
+        z_wait(1, step)
+        send_on(1, step + 1)
         for t in (0, 1):
-            z_wait(t, step)
-            if step < hz:
-                z_start(t, step + 1)
-            if step == 1 and t == 0:
-                state_in()
-                metas_in()
-        if step < hz:
-            if step <= hy:
-                y_wait(step)
-                done_y = step
-                if step < hy:
-                    y_start(step + 1)
-            for t in (0, 1):
-                pack(step, t)
-                x_start(step, t)
+            pack(step, t)
+            x_start(step, t)
+        done_y += 1
+        y_next(done_y)
+    if hz == 2:
+        state_in()
     while done_y < hy:
         done_y += 1
-        y_wait(done_y)
-        if done_y < hy:
-            y_start(done_y + 1)
-    for t in (0, 1):
-        pack(0, t)
-        x_start(0, t)
-    for p in list(range(1, hz)) + [0]:
+        y_next(done_y)
+
+    def work(p):
         for t in (0, 1):
             x_wait(p, t)
         compute(p)
         r_start(p)
+
+    early = list(range(1, hz - 1))
+    if early:
+        work(early[0])
+    z_wait(0, hz - 1)
+    z_start(0, hz)
+    pack(hz - 1, 0)
+    x_start(hz - 1, 0)
+    for p in early[1:]:
+        work(p)
+    z_wait(1, hz - 1)
+    z_start(1, hz)
+    pack(hz - 1, 1)
+    x_start(hz - 1, 1)
+    for t in (0, 1):
+        z_wait(t, hz)
+        pack(0, t)
+        x_start(0, t)
+    for p in early[:1]:
+        relay(p)
+    work(hz - 1)
+    for p in early[1:]:
+        relay(p)
+    work(0)
     rs_step(1)
-    for p in list(range(1, hz)):
-        relay(p)
+    relay(hz - 1)
     if hy > 1:
         rs_step(2)
     relay(0)
@@ -445,6 +525,9 @@
         scratch_shapes=[
             pltpu.VMEM((NZ * rows, width), BF16),
             pltpu.VMEM((NZ * rows, width), BF16),
+            pltpu.VMEM((2, 2, chunk // 2 + chunk // 4, width), BF16),
+            pltpu.VMEM((2, 2, chunk // 2 + chunk // 4, width), BF16),
+            pltpu.VMEM((2, chunk // 2, width), BF16),
             pltpu.VMEM((NZ * 8, rows), F32),
             pltpu.VMEM((part, both), BF16),
             pltpu.VMEM((width, both), BF16),

time: 190 us -> 190 us (level)
  no operation moved by 1% of the time
where the time goes in v2:
time: 190 us
  Pallas kernels  176 us (93%)
  other arithmetic  6.03 us (3%)
  local copies, waits for them, and re-layouts  5.66 us (3%)
  between operations  2 us (1%)
    pallas_call x1, Pallas kernels, exchange(): pl.pallas_call(functools.partial(kernel, (ny, rows, width, hidden, wide))...  176 us
    broadcast_in_dim x1, other arithmetic, shards(): return (token_grad, weight_grad, w_new[None], m_new[None], v_new[None])  4.1 us

profile of v2, /device:TPU:1, one launch (start us, length us, event | category | flops | bytes accessed | tf_op | source)
XLA Modules:
  0.0 190.1 jit_solution(12928945589905227418)
XLA Ops:
  0.6 0.0 copy-start.5
  0.7 0.6 copy-done.5
  1.3 0.6 fusion.10
  3.2 0.0 copy-start.6
  3.2 0.6 copy-done.6
  3.9 0.1 select_reduce_fusion
  4.0 0.0 copy-start.3
  4.0 0.1 pad.2.clone
  4.1 0.6 copy-done.3
  4.7 0.0 copy-start.4
  4.7 0.7 copy-done.4
  5.3 0.7 maximum_maximum_fusion.meta
  6.0 0.7 broadcast_in_dim.43.homec
  6.7 0.6 broadcast_in_dim.45.flag
  7.3 0.0 copy-start
  7.3 0.0 copy-start.1
  7.3 176.4 %exchange.1 = (bf16[128,2048]{1,0:T(8,128)(2,1)}, f32[128,128]{1,0:T(8,128)}, f32[256,1024]{1,0:T(8,128)}, bf16[256,1024]{1,0:T(8,128)(2,1)}, bf16[256,1024]{1,0:T(8,128)(2,1)}, /*index=5*/bf16[256,1024]{1,0:T(8,128)(2,1)}) custom-call(bf16[128,2048]{1,0:T(8,128)(2,1)} %tok.1, bf16[128,2048]{1,0:T(8,128)(2,1)} %up.1, f32[8,128]{1,0:T(8,128)} %maximum_maximum_fusion.meta, ...), custom_call_target="tpu_custom_call" | custom-call | tf_op jit(solution)/shard_map/exchange/pallas_call | solution.py:512
  183.8 0.9 copy.15
  184.7 0.5 fusion.9
  185.2 0.0 copy-done
  185.2 0.0 copy-done.1
  185.2 0.0 copy-start.2
  185.2 4.1 %fusion.6 = (bf16[1,256,1024]{2,1,0:T(8,128)(2,1)}, bf16[1,256,1024]{2,1,0:T(8,128)(2,1)}, bf16[1,256,1024]{2,1,0:T(8,128)(2,1)}) fusion(f32[256,1024]{1,0:T(8,128)} %get-tuple-element.15, bf16[256,1024]{1,0:T(8,128)(2,1)} %get-tuple-element.16, pred[]{:T(512)S(6)} %eq.39, bf16[1,256,1024]{2,1,0:T(8,128)(2,1)S(1)} %copy-done.1, ...), kind=kLoop, calls=%fused_computation.10 | loop fusion | flops 5767168 | bytes 5242881 | tf_op jit(solution)/shard_map/broadcast_in_dim | solution.py:605
  189.3 0.0 copy-done.2
  189.3 0.8 copy.17
  (5 shorter events, 0.0 us)
Async XLA Ops:
  0.6 0.7 copy-start.5
  3.2 0.7 copy-start.6
  4.0 0.7 copy-start.3
  4.7 0.7 copy-start.4
  7.3 177.9 %copy-start = (bf16[1,256,1024]{2,1,0:T(8,128)(2,1)S(1)}, bf16[1,256,1024]{2,1,0:T(8,128)(2,1)}, u32[]{:S(2)}) copy-start(bf16[1,256,1024]{2,1,0:T(8,128)(2,1)} %param.16) | copy-start | bytes 1572868
  7.3 177.9 %copy-start.1 = (bf16[1,256,1024]{2,1,0:T(8,128)(2,1)S(1)}, bf16[1,256,1024]{2,1,0:T(8,128)(2,1)}, u32[]{:S(2)}) copy-start(bf16[1,256,1024]{2,1,0:T(8,128)(2,1)} %param.17) | copy-start | bytes 1572868
  185.2 4.1 %copy-start.2 = (bf16[128,2048]{1,0:T(8,128)(2,1)S(1)}, bf16[128,2048]{1,0:T(8,128)(2,1)}, u32[]{:S(2)}) copy-start(bf16[128,2048]{1,0:T(8,128)(2,1)} %get-tuple-element.25) | copy-start | bytes 1572868

commit v3 on v2

--- a/solution.py
+++ b/solution.py
@@ -37,8 +37,8 @@
 
 def kernel(
     sizes,
-    tok, up, meta, homec, flag, w_in, m_in, v_in,
-    tg, dwo, grad, w_sel, m_got, v_got,
+    tok, up, ids, gate, place_row, swap_row, w_in, m_in, v_in,
+    tg, dwo, grad, w_sel, flag, m_got, v_got,
     xa, ya, p3, r3, r4, mt, w_got, wfull, sx, sy, rx, ry, act_all, dh_all,
     dxs, dr, sr, fr, rs_send, rs_recv,
     z_send, z_recv, mt_send, mt_recv, sw_send, sw_recv, y_send, y_recv,
@@ -137,18 +137,27 @@
         return remote(ref, ref, mt_send.at[k - 1], mt_recv.at[k - 1], zdev(k))
 
     def positions():
-        experts = homec.shape[0]
-        ids0, ids1 = meta[0:1, :], meta[1:2, :]
-        each = iota((experts, rows), 0).astype(F32)
-        one0, one1 = ids0 == each, ids1 == each
+        experts = place_row.shape[1]
+        pairs = experts // 2
+        spread = jnp.where(iota((experts, experts), 0) == iota((experts, experts), 1), place_row[...], 0)
+        place = jnp.sum(spread.astype(F32), 1, keepdims=True).astype(jnp.int32)
+        low = jnp.where(place >= pairs, place - pairs, place)
+        trade = jnp.where(iota((experts, pairs), 1) == low, swap_row[...], 0)
+        moved = jnp.sum(trade.astype(F32), 1, keepdims=True) == 1.0
+        home = jnp.where(moved, jnp.where(place >= pairs, place - pairs, place + pairs), place).astype(F32)
+        mine = jnp.where(iota((8, pairs), 1) == lax.rem(e, pairs), swap_row[...], 0)
+        flag[...] = jnp.broadcast_to(jnp.sum(mine.astype(F32), 1, keepdims=True), flag.shape)
+        each = iota((experts, rows), 0)
+        one0, one1 = ids[0:1, :] == each, ids[1:2, :] == each
         named = jnp.where(one0 | one1, 1.0, 0.0).astype(BF16)
         before = jnp.where(iota((rows, rows), 0) < iota((rows, rows), 1), 1.0, 0.0).astype(BF16)
-        earlier = jnp.dot(named, before, preferred_element_type=F32)
-        place = homec[...] * CAP + earlier
-        pos0 = jnp.sum(jnp.where(one0, place, 0.0), 0, keepdims=True)
-        pos1 = jnp.sum(jnp.where(one1, place, 0.0), 0, keepdims=True)
+        spot = home * CAP + jnp.dot(named, before, preferred_element_type=F32)
+        pos0 = jnp.sum(jnp.where(one0, spot, 0.0), 0, keepdims=True)
+        pos1 = jnp.sum(jnp.where(one1, spot, 0.0), 0, keepdims=True)
         line = iota((8, rows), 0)
-        tile = jnp.where(line == 0, pos0, jnp.where(line == 1, pos1, meta[...]))
+        gates = gate[...].astype(F32)
+        tile = jnp.where(line == 2, gates[0:1, :], gates[1:2, :])
+        tile = jnp.where(line == 0, pos0, jnp.where(line == 1, pos1, tile))
         mt[pl.ds(pl.multiple_of(z * 8, 8), 8), :] = tile
 
     def sources(p):
@@ -359,14 +368,11 @@
             tg[:, cols] = lax.dot_general(both, fr[:, cols], dims, preferred_element_type=F32).astype(BF16)
 
         tiles(width, 512, body)
-        lane = iota((rows, LANES), 1)
-        sums = [
-            lax.dot_general(
-                jnp.where(hit, 1.0, 0.0).astype(BF16), fr[:, width:], dims, preferred_element_type=F32
+        for k, hit in enumerate((hit0, hit1)):
+            sums = lax.dot_general(
+                fr[:, width:], jnp.where(hit, 1.0, 0.0).astype(BF16), dims, preferred_element_type=F32
             )
-            for hit in (hit0, hit1)
-        ]
-        dwo[...] = jnp.where(lane == 0, sums[0], sums[1])
+            dwo[k : k + 1, :] = (sums[0:1, :] / tile[2 + k : 3 + k, :]).astype(BF16)
 
     def metas_in():
         for k in range(1, NZ):
@@ -379,19 +385,22 @@
         wfull[here, :] = chosen
         w_sel[...] = chosen
         y_start(1)
-        swaps[1].start()
-        swaps[2].start()
-
-    def y_next(step):
+
+    y_step = [0]
+
+    def y_next():
+        step = y_step[0] = y_step[0] + 1
         if step <= hy:
             y_wait(step)
             if step < hy:
                 y_start(step + 1)
 
-    def first_copies():
+    def metas_out():
         positions()
         for k in range(1, NZ):
             mt_copy(k, True).start()
+
+    def own_rows():
         xa[pl.ds(pl.multiple_of(z * rows, rows), rows), :] = tok[...]
         ya[pl.ds(pl.multiple_of(z * rows, rows), rows), :] = up[...]
 
@@ -400,74 +409,82 @@
             pack_ahead(t)
         z_start(t, step)
 
-    swaps[0].start()
-    if hz > 2:
-        z_start(0, 1)
-        z_start(1, 1)
-        first_copies()
-    else:
-        first_copies()
-        metas_in()
-        send_on(0, 1)
-        send_on(1, 1)
-    done_y = 0
-    for step in range(1, hz - 1):
-        z_wait(0, step)
-        if step == 1:
-            metas_in()
-        send_on(0, step + 1)
-        if step == 1:
-            state_in()
-        else:
-            done_y += 1
-            y_next(done_y)
-        z_wait(1, step)
-        send_on(1, step + 1)
-        for t in (0, 1):
-            pack(step, t)
-            x_start(step, t)
-        done_y += 1
-        y_next(done_y)
-    if hz == 2:
-        state_in()
-    while done_y < hy:
-        done_y += 1
-        y_next(done_y)
+    def dispatch(p, t):
+        pack(p, t)
+        x_start(p, t)
 
     def work(p):
         for t in (0, 1):
             x_wait(p, t)
         compute(p)
-        r_start(p)
-
+
+    swaps[0].start()
+    if hz > 2:
+        z_start(0, 1)
+        metas_out()
+        z_start(1, 1)
+        own_rows()
+    else:
+        metas_out()
+        own_rows()
+        metas_in()
+        send_on(0, 1)
+        send_on(1, 1)
+        state_in()
+        swaps[1].start()
+        swaps[2].start()
+    for step in range(1, hz - 1):
+        z_wait(0, step)
+        if step == 2:
+            send_on(0, step + 1)
+            y_next()
+        else:
+            send_on(0, step + 1)
+            state_in()
+            swaps[1].start()
+        z_wait(1, step)
+        send_on(1, step + 1)
+        if step == 1:
+            y_next()
+            metas_in()
+        dispatch(step, 0)
+        dispatch(step, 1)
+        if step == 1:
+            swaps[2].start()
+        else:
+            y_next()
     early = list(range(1, hz - 1))
+    z_wait(0, hz - 1)
+    z_start(0, hz)
+    dispatch(hz - 1, 0)
+    while y_step[0] < hy:
+        y_next()
     if early:
         work(early[0])
-    z_wait(0, hz - 1)
-    z_start(0, hz)
-    pack(hz - 1, 0)
-    x_start(hz - 1, 0)
+    z_wait(1, hz - 1)
+    z_start(1, hz)
+    dispatch(hz - 1, 1)
     for p in early[1:]:
         work(p)
-    z_wait(1, hz - 1)
-    z_start(1, hz)
-    pack(hz - 1, 1)
-    x_start(hz - 1, 1)
+        r_start(p)
     for t in (0, 1):
         z_wait(t, hz)
-        pack(0, t)
-        x_start(0, t)
-    for p in early[:1]:
+        dispatch(0, t)
+    for p in early[1:]:
         relay(p)
     work(hz - 1)
-    for p in early[1:]:
-        relay(p)
+    r_start(hz - 1)
     work(0)
+    r_start(0)
+    for p in early[:1]:
+        r_start(p)
     rs_step(1)
     relay(hz - 1)
     if hy > 1:
         rs_step(2)
     relay(0)
+    for p in early[:1]:
+        relay(p)
     for step in range(3, hy + 1):
         rs_step(step)
     finish()
@@ -496,7 +513,7 @@
         swaps[i].wait()
 
 
-def exchange(tokens, upstream, meta, homec, flag, w_in, m_in, v_in):
+def exchange(tokens, upstream, ids, gate, place, swap, w_in, m_in, v_in):
     ny = lax.axis_size("dp")
     rows, width = tokens.shape
     part, both = w_in.shape
@@ -514,14 +531,15 @@
         name="exchange",
         out_shape=(
             jax.ShapeDtypeStruct((rows, width), BF16),
-            jax.ShapeDtypeStruct((rows, LANES), F32),
+            jax.ShapeDtypeStruct((2, rows), BF16),
             jax.ShapeDtypeStruct((part, both), F32),
             jax.ShapeDtypeStruct((part, both), BF16),
+            jax.ShapeDtypeStruct((8, both), F32),
             jax.ShapeDtypeStruct((part, both), BF16),
             jax.ShapeDtypeStruct((part, both), BF16),
         ),
-        in_specs=[vmem] * 6 + [any_] * 2,
-        out_specs=(vmem,) * 4 + (any_,) * 2,
+        in_specs=[vmem] * 7 + [any_] * 2,
+        out_specs=(vmem,) * 5 + (any_,) * 2,
         scratch_shapes=[
             pltpu.VMEM((NZ * rows, width), BF16),
             pltpu.VMEM((NZ * rows, width), BF16),
@@ -556,7 +574,7 @@
         compiler_params=pltpu.CompilerParams(
             collective_id=0, has_side_effects=True, vmem_limit_bytes=60 * 1024 * 1024
         ),
-    )(tokens, upstream, meta, homec, flag, w_in, m_in, v_in)
+    )(tokens, upstream, ids, gate, place, swap, w_in, m_in, v_in)
 
 
 def adam_update(weights, first, second, grad):
@@ -579,30 +597,15 @@
     first_moment,
     second_moment,
 ):
-    lanes_count = lax.axis_size("expert")
-    half = lanes_count // 2
-    rows, top = expert_ids.shape
-    both = expert_state.shape[2]
-    halves = jnp.arange(half, dtype=jnp.int32)
-    own_index = lax.axis_index("expert")
-    own_flag = jnp.sum(jnp.where(halves == own_index % half, swap_pair, 0))
-    match_half = (placement % half)[:, None] == halves[None, :]
-    moved = jnp.sum(jnp.where(match_half, swap_pair[None, :], 0), 1)
-    home = jnp.where(moved == 1, placement ^ half, placement)
-    homec = jnp.broadcast_to(home.astype(F32)[:, None], (lanes_count, rows))
-    flag = jnp.broadcast_to(own_flag.astype(F32), (8, both))
-    meta = jnp.concatenate(
-        [expert_ids.T.astype(F32), route_weight.T.astype(F32), jnp.zeros((8 - 2 * top, rows), F32)], 0
+    token_grad, weight_grad, grad, w_sel, flag, m_got, v_got = exchange(
+        tokens, upstream, expert_ids.T, route_weight.T, placement[None], swap_pair[None],
+        expert_state[0], first_moment[0], second_moment[0],
     )
-    token_grad, weighted, grad, w_sel, m_got, v_got = exchange(
-        tokens, upstream, meta, homec, flag, expert_state[0], first_moment[0], second_moment[0]
-    )
-    weight_grad = (weighted[:, :top] / route_weight.astype(F32)).astype(BF16)
-    swapped = own_flag == 1
+    swapped = flag[0:1] == 1.0
     m_sel = jnp.where(swapped, m_got, first_moment[0])
     v_sel = jnp.where(swapped, v_got, second_moment[0])
     w_new, m_new, v_new = adam_update(w_sel, m_sel, v_sel, grad)
-    return (token_grad, weight_grad, w_new[None], m_new[None], v_new[None])
+    return (token_grad, weight_grad.T, w_new[None], m_new[None], v_new[None])
 
 
 def solution(mesh):

time: 190 us -> 167 us (0.88)
  Pallas kernels: 176 us -> 160 us
  local copies, waits for them, and re-layouts: 5.66 us -> 1.32 us
    pallas_call x1, Pallas kernels: 176 us -> 160 us  [exchange(): pl.pallas_call(functools.partial(kernel, (ny, rows, width, hidden, wide))...]
    unnamed x15 -> x10, local copies, waits for them, and re-layouts: 3.35 us -> 1.32 us
where the time goes in v3:
time: 167 us
  Pallas kernels  160 us (96%)
  other arithmetic  4.87 us (3%)
    pallas_call x1, Pallas kernels, exchange(): pl.pallas_call(functools.partial(kernel, (ny, rows, width, hidden, wide))...  160 us
    broadcast_in_dim x1, other arithmetic, shards(): return (token_grad, weight_grad.T, w_new[None], m_new[None], v_new[None])  4.08 us

profile of v3, /device:TPU:1, one launch (start us, length us, event | category | flops | bytes accessed | tf_op | source)
XLA Modules:
  0.0 166.8 jit_solution(1471435608207832411)
XLA Ops:
  0.6 0.0 copy-start
  0.6 0.0 copy-start.1
  0.7 159.9 %exchange.1 = (bf16[128,2048]{1,0:T(8,128)(2,1)}, bf16[2,128]{1,0:T(2,128)(2,1)}, f32[256,1024]{1,0:T(8,128)}, bf16[256,1024]{1,0:T(8,128)(2,1)}, f32[8,1024]{1,...) custom-call(bf16[128,2048]{1,0:T(8,128)(2,1)} %tok.1, bf16[128,2048]{1,0:T(8,128)(2,1)} %up.1, ...), custom_call_target="tpu_custom_call" | custom-call | tf_op jit(solution)/shard_map/exchange/pallas_call | solution.py:529
  160.5 0.8 compare_reduce_fusion
  161.3 0.0 copy-done
  161.3 0.0 copy-done.1
  161.3 0.0 copy-start.2
  161.4 4.1 %fusion.6 = (bf16[1,256,1024]{2,1,0:T(8,128)(2,1)}, bf16[1,256,1024]{2,1,0:T(8,128)(2,1)}, bf16[1,256,1024]{2,1,0:T(8,128)(2,1)}) fusion(f32[256,1024]{1,0:T(8,128)} %get-tuple-element.17, bf16[256,1024]{1,0:T(8,128)(2,1)} %get-tuple-element.18, pred[1024]{0:T(1024)(128)(4,1)S(1)} %compare_reduce_fusion, bf16[1,256,1024]{2,1,0:T(8,128)(2,1)S(1)} %copy-done.1, ...), kind=kLoop, calls=%fused_computation.10 | loop fusion | flops 5767168 | bytes 5243904 | tf_op jit(solution)/shard_map/broadcast_in_dim | solution.py:608
  165.4 0.0 copy-done.2
  165.4 0.0 copy-start.3
  165.4 0.8 copy.16
  166.2 0.0 copy-done.3
  166.2 0.5 copy.17
Async XLA Ops:
  0.6 160.7 %copy-start = (bf16[1,256,1024]{2,1,0:T(8,128)(2,1)S(1)}, bf16[1,256,1024]{2,1,0:T(8,128)(2,1)}, u32[]{:S(2)}) copy-start(bf16[1,256,1024]{2,1,0:T(8,128)(2,1)} %param.16) | copy-start | bytes 1572868
  0.6 160.7 %copy-start.1 = (bf16[1,256,1024]{2,1,0:T(8,128)(2,1)S(1)}, bf16[1,256,1024]{2,1,0:T(8,128)(2,1)}, u32[]{:S(2)}) copy-start(bf16[1,256,1024]{2,1,0:T(8,128)(2,1)} %param.17) | copy-start | bytes 1572868
  161.3 4.1 %copy-start.2 = (bf16[128,2048]{1,0:T(8,128)(2,1)S(1)}, bf16[128,2048]{1,0:T(8,128)(2,1)}, u32[]{:S(2)}) copy-start(bf16[128,2048]{1,0:T(8,128)(2,1)} %get-tuple-element.27) | copy-start | bytes 1572868
  165.4 0.8 copy-start.3

commit v4 on v3

--- a/solution.py
+++ b/solution.py
@@ -419,72 +419,56 @@
         compute(p)
 
     swaps[0].start()
-    if hz > 2:
-        z_start(0, 1)
-        metas_out()
-        z_start(1, 1)
-        own_rows()
-    else:
-        metas_out()
-        own_rows()
-        metas_in()
-        send_on(0, 1)
-        send_on(1, 1)
-        state_in()
-        swaps[1].start()
-        swaps[2].start()
-    for step in range(1, hz - 1):
-        z_wait(0, step)
-        if step == 2:
-            send_on(0, step + 1)
-            y_next()
-        else:
-            send_on(0, step + 1)
-            state_in()
-            swaps[1].start()
-        z_wait(1, step)
-        send_on(1, step + 1)
-        if step == 1:
-            y_next()
-            metas_in()
-        dispatch(step, 0)
-        dispatch(step, 1)
-        if step == 1:
-            swaps[2].start()
-        else:
-            y_next()
-    early = list(range(1, hz - 1))
-    z_wait(0, hz - 1)
-    z_start(0, hz)
-    dispatch(hz - 1, 0)
+    z_start(0, 1)
+    metas_out()
+    own_rows()
+    z_wait(0, 1)
+    send_on(0, 2)
+    send_on(1, 1)
+    state_in()
+    metas_in()
+    dispatch(1, 0)
+    swaps[1].start()
+    z_wait(0, 2)
+    send_on(0, 3)
+    y_next()
+    dispatch(2, 0)
+    z_wait(1, 1)
+    send_on(1, 2)
+    dispatch(1, 1)
+    swaps[2].start()
+    y_next()
+    z_wait(0, 3)
+    send_on(0, 4)
+    dispatch(3, 0)
+    y_next()
+    z_wait(1, 2)
+    send_on(1, 3)
+    dispatch(2, 1)
+    z_wait(0, 4)
+    dispatch(0, 0)
     while y_step[0] < hy:
         y_next()
-    if early:
-        work(early[0])
-    z_wait(1, hz - 1)
-    z_start(1, hz)
-    dispatch(hz - 1, 1)
-    for p in early[1:]:
-        work(p)
-        r_start(p)
-    for t in (0, 1):
-        z_wait(t, hz)
-        dispatch(0, t)
-    for p in early[1:]:
-        relay(p)
-    work(hz - 1)
-    r_start(hz - 1)
+    work(1)
+    work(2)
+    r_start(2)
+    z_wait(1, 3)
+    send_on(1, 4)
+    dispatch(3, 1)
+    z_wait(1, 4)
+    dispatch(0, 1)
+    relay(2)
+    work(3)
+    r_start(3)
     work(0)
     r_start(0)
-    for p in early[:1]:
-        r_start(p)
+    r_start(1)
     rs_step(1)
-    relay(hz - 1)
+    relay(3)
     if hy > 1:
         rs_step(2)
     relay(0)
-    for p in early[:1]:
-        relay(p)
+    relay(1)
     for step in range(3, hy + 1):
         rs_step(step)
     finish()

time: 167 us -> 167 us (level)
  no operation moved by 1% of the time
where the time goes in v4:
time: 167 us; the launch traced here: 166 us
  Pallas kernels  160 us (96%)
  other arithmetic  4.87 us (3%)
    pallas_call x1, Pallas kernels, exchange(): pl.pallas_call(functools.partial(kernel, (ny, rows, width, hidden, wide))...  160 us
    broadcast_in_dim x1, other arithmetic, shards(): return (token_grad, weight_grad.T, w_new[None], m_new[None], v_new[None])  4.08 us

profile of v4, /device:TPU:1, one launch (start us, length us, event | category | flops | bytes accessed | tf_op | source)
XLA Modules:
  0.0 166.4 jit_solution(15523074657849944070)
XLA Ops:
  0.6 0.0 copy-start
  0.6 0.0 copy-start.1
  0.7 159.6 %exchange.1 = (bf16[128,2048]{1,0:T(8,128)(2,1)}, bf16[2,128]{1,0:T(2,128)(2,1)}, f32[256,1024]{1,0:T(8,128)}, bf16[256,1024]{1,0:T(8,128)(2,1)}, f32[8,1024]{1,...) custom-call(bf16[128,2048]{1,0:T(8,128)(2,1)} %tok.1, bf16[128,2048]{1,0:T(8,128)(2,1)} %up.1, ...), custom_call_target="tpu_custom_call" | custom-call | tf_op jit(solution)/shard_map/exchange/pallas_call | solution.py:513
  160.2 0.8 compare_reduce_fusion
  161.0 0.0 copy-done
  161.0 0.0 copy-done.1
  161.0 0.0 copy-start.2
  161.0 4.1 %fusion.6 = (bf16[1,256,1024]{2,1,0:T(8,128)(2,1)}, bf16[1,256,1024]{2,1,0:T(8,128)(2,1)}, bf16[1,256,1024]{2,1,0:T(8,128)(2,1)}) fusion(f32[256,1024]{1,0:T(8,128)} %get-tuple-element.17, bf16[256,1024]{1,0:T(8,128)(2,1)} %get-tuple-element.18, pred[1024]{0:T(1024)(128)(4,1)S(1)} %compare_reduce_fusion, bf16[1,256,1024]{2,1,0:T(8,128)(2,1)S(1)} %copy-done.1, ...), kind=kLoop, calls=%fused_computation.10 | loop fusion | flops 5767168 | bytes 5243904 | tf_op jit(solution)/shard_map/broadcast_in_dim | solution.py:592
  165.1 0.0 copy-done.2
  165.1 0.0 copy-start.3
  165.1 0.8 copy.16
  165.9 0.0 copy-done.3
  165.9 0.5 copy.17
Async XLA Ops:
  0.6 160.4 %copy-start = (bf16[1,256,1024]{2,1,0:T(8,128)(2,1)S(1)}, bf16[1,256,1024]{2,1,0:T(8,128)(2,1)}, u32[]{:S(2)}) copy-start(bf16[1,256,1024]{2,1,0:T(8,128)(2,1)} %param.16) | copy-start | bytes 1572868
  0.6 160.4 %copy-start.1 = (bf16[1,256,1024]{2,1,0:T(8,128)(2,1)S(1)}, bf16[1,256,1024]{2,1,0:T(8,128)(2,1)}, u32[]{:S(2)}) copy-start(bf16[1,256,1024]{2,1,0:T(8,128)(2,1)} %param.17) | copy-start | bytes 1572868
  161.0 4.1 %copy-start.2 = (bf16[128,2048]{1,0:T(8,128)(2,1)S(1)}, bf16[128,2048]{1,0:T(8,128)(2,1)}, u32[]{:S(2)}) copy-start(bf16[128,2048]{1,0:T(8,128)(2,1)} %get-tuple-element.27) | copy-start | bytes 1572868
  165.1 0.8 copy-start.3

commit v5 on v4

--- a/solution.py
+++ b/solution.py
@@ -326,19 +326,18 @@
     def rs_halves(way, step):
         return (way,) if step == 1 else (0, 1)
 
-    def rs_step(step):
-        for h in (0, 1):
-            for way in (0, 1):
-                if h not in rs_halves(way, step):
-                    continue
-                sign = 1 if way == 0 else -1
-                block = lax.rem(d + sign * (hy + 1 - step) + ny, ny)
-                total = own_part(block, h)
-                if step > 1 and h in rs_halves(way, step - 1):
-                    rs_copy(way, step - 1, h).wait_recv()
-                    total += rs_recv[way, step - 2, h].astype(F32)
-                rs_send[way, step - 1, h] = total.astype(BF16)
-                rs_copy(way, step, h).start()
+    def rs_some(step, some):
+        for way, h in some:
+            sign = 1 if way == 0 else -1
+            block = lax.rem(d + sign * (hy + 1 - step) + ny, ny)
+            total = own_part(block, h)
+            if step > 1 and h in rs_halves(way, step - 1):
+                rs_copy(way, step - 1, h).wait_recv()
+                total += rs_recv[way, step - 2, h].astype(F32)
+            rs_send[way, step - 1, h] = total.astype(BF16)
+            rs_copy(way, step, h).start()
+
+    fresh, begun = ((0, 1), (1, 0)), ((0, 0), (1, 1))
 
     def rs_last():
         for h in (0, 1):
@@ -463,14 +462,19 @@
     work(0)
     r_start(0)
     r_start(1)
-    rs_step(1)
+    rs_some(1, begun)
+    if hy > 1:
+        rs_some(2, fresh)
     relay(3)
     if hy > 1:
-        rs_step(2)
+        rs_some(2, begun)
     relay(0)
-    relay(1)
     for step in range(3, hy + 1):
-        rs_step(step)
+        rs_some(step, fresh + begun)
+        if step == 3:
+            relay(1)
+    if hy < 3:
+        relay(1)
     finish()
     rs_last()
 

time: 167 us -> 166 us (level)
  no operation moved by 1% of the time
where the time goes in v5:
time: 166 us; the launch traced here: 165 us
  Pallas kernels  159 us (96%)
  other arithmetic  4.87 us (3%)
    pallas_call x1, Pallas kernels, exchange(): pl.pallas_call(functools.partial(kernel, (ny, rows, width, hidden, wide))...  159 us
    broadcast_in_dim x1, other arithmetic, shards(): return (token_grad, weight_grad.T, w_new[None], m_new[None], v_new[None])  4.08 us

profile of v5, /device:TPU:1, one launch (start us, length us, event | category | flops | bytes accessed | tf_op | source)
XLA Modules:
  0.0 165.4 jit_solution(5412676595881453376)
XLA Ops:
  0.6 0.0 copy-start
  0.6 0.0 copy-start.1
  0.7 158.5 %exchange.1 = (bf16[128,2048]{1,0:T(8,128)(2,1)}, bf16[2,128]{1,0:T(2,128)(2,1)}, f32[256,1024]{1,0:T(8,128)}, bf16[256,1024]{1,0:T(8,128)(2,1)}, f32[8,1024]{1,...) custom-call(bf16[128,2048]{1,0:T(8,128)(2,1)} %tok.1, bf16[128,2048]{1,0:T(8,128)(2,1)} %up.1, ...), custom_call_target="tpu_custom_call" | custom-call | tf_op jit(solution)/shard_map/exchange/pallas_call | solution.py:517
  159.2 0.8 compare_reduce_fusion
  160.0 0.0 copy-done
  160.0 0.0 copy-done.1
  160.0 0.0 copy-start.2
  160.0 4.1 %fusion.6 = (bf16[1,256,1024]{2,1,0:T(8,128)(2,1)}, bf16[1,256,1024]{2,1,0:T(8,128)(2,1)}, bf16[1,256,1024]{2,1,0:T(8,128)(2,1)}) fusion(f32[256,1024]{1,0:T(8,128)} %get-tuple-element.17, bf16[256,1024]{1,0:T(8,128)(2,1)} %get-tuple-element.18, pred[1024]{0:T(1024)(128)(4,1)S(1)} %compare_reduce_fusion, bf16[1,256,1024]{2,1,0:T(8,128)(2,1)S(1)} %copy-done.1, ...), kind=kLoop, calls=%fused_computation.10 | loop fusion | flops 5767168 | bytes 5243904 | tf_op jit(solution)/shard_map/broadcast_in_dim | solution.py:596
  164.1 0.0 copy-done.2
  164.1 0.0 copy-start.3
  164.1 0.8 copy.16
  164.9 0.0 copy-done.3
  164.9 0.5 copy.17
Async XLA Ops:
  0.6 159.3 %copy-start = (bf16[1,256,1024]{2,1,0:T(8,128)(2,1)S(1)}, bf16[1,256,1024]{2,1,0:T(8,128)(2,1)}, u32[]{:S(2)}) copy-start(bf16[1,256,1024]{2,1,0:T(8,128)(2,1)} %param.16) | copy-start | bytes 1572868
  0.6 159.3 %copy-start.1 = (bf16[1,256,1024]{2,1,0:T(8,128)(2,1)S(1)}, bf16[1,256,1024]{2,1,0:T(8,128)(2,1)}, u32[]{:S(2)}) copy-start(bf16[1,256,1024]{2,1,0:T(8,128)(2,1)} %param.17) | copy-start | bytes 1572868
  160.0 4.1 %copy-start.2 = (bf16[128,2048]{1,0:T(8,128)(2,1)S(1)}, bf16[128,2048]{1,0:T(8,128)(2,1)}, u32[]{:S(2)}) copy-start(bf16[128,2048]{1,0:T(8,128)(2,1)} %get-tuple-element.27) | copy-start | bytes 1572868
  164.1 0.8 copy-start.3
